TPU v7x, 32 devices: a whole 2x2x4 slice. The times are simulated.
32 devices in a mesh: dp: 8 (over z, y), tensor: 4 (over x, core).
Axes of the slice: x: 2, y: 2, z: 4, core: 2. Of those that a mesh axis runs over, the one named last changes fastest.
Arguments:
- layer_in: bfloat16 [4096, 768], P(('dp', 'tensor')), may hold values from -6 to 6
- encoder_states: bfloat16 [4096, 768], P(('dp', 'tensor')), may hold values from -6 to 6
- grad_out: bfloat16 [4096, 768], P(('dp', 'tensor')), may hold values from -6 to 6
- buckets: int32 [8, 512, 512], P('dp'), may hold values from 0 to 31, as said below
- keep: int32 [8, 512, 512], P('dp'), may hold values from 0 to 1, as said below
- wq_self: bfloat16 [768, 768], P('dp', 'tensor'), may hold values from -0.02734375 to 0.02734375
- wk_self: bfloat16 [768, 768], P('dp', 'tensor'), may hold values from -0.21875 to 0.21875
- wv_self: bfloat16 [768, 768], P('dp', 'tensor'), may hold values from -0.21875 to 0.21875
- wo_self: bfloat16 [768, 768], P('tensor', 'dp'), may hold values from -0.875 to 0.875
- wq_cross: bfloat16 [768, 768], P('dp', 'tensor'), may hold values from -0.02734375 to 0.02734375
- wk_cross: bfloat16 [768, 768], P('dp', 'tensor'), may hold values from -0.21875 to 0.21875
- wv_cross: bfloat16 [768, 768], P('dp', 'tensor'), may hold values from -0.21875 to 0.21875
- wo_cross: bfloat16 [768, 768], P('tensor', 'dp'), may hold values from -0.875 to 0.875
- w_gate: bfloat16 [768, 2048], P('dp', 'tensor'), may hold values from -0.21875 to 0.21875
- w_up: bfloat16 [768, 2048], P('dp', 'tensor'), may hold values from -0.21875 to 0.21875
- w_down: bfloat16 [2048, 768], P('tensor', 'dp'), may hold values from -0.125 to 0.125
- norm_scales: bfloat16 [3, 768], P(None, 'dp'), may hold values from 0.5 to 1.5
- rel_bias: float32 [32, 12], P(None, 'tensor'), may hold values from -4 to 4
Outputs:
- layer_out: bfloat16 [4096, 768], P(('dp', 'tensor'))
- grad_in: float32 [4096, 768], P(('dp', 'tensor'))
- grad_encoder: float32 [4096, 768], P(('dp', 'tensor'))
- grad_wq_self: float32 [768, 768], P('dp', 'tensor')
- grad_wk_self: float32 [768, 768], P('dp', 'tensor')
- grad_wv_self: float32 [768, 768], P('dp', 'tensor')
- grad_wo_self: float32 [768, 768], P('tensor', 'dp')
- grad_wq_cross: float32 [768, 768], P('dp', 'tensor')
- grad_wk_cross: float32 [768, 768], P('dp', 'tensor')
- grad_wv_cross: float32 [768, 768], P('dp', 'tensor')
- grad_wo_cross: float32 [768, 768], P('tensor', 'dp')
- grad_w_gate: float32 [768, 2048], P('dp', 'tensor')
- grad_w_up: float32 [768, 2048], P('dp', 'tensor')
- grad_w_down: float32 [2048, 768], P('tensor', 'dp')
- grad_norm_scales: float32 [3, 768], P(None, ('dp', 'tensor'))
- grad_rel_bias: float32 [32, 12], P(None, 'tensor')
Inputs may be any that keep to these rules, and one draw needn't show every extreme that they name: Each sequence holds one to three documents, the first of 256 positions or more. buckets[s, i, j] is the T5 bucket (exact below 16, logarithmic up to distance 128, the last bucket beyond) of i - j where keep = 1, and 0 elsewhere. keep[s, i, j] = 1 exactly where key j lies in the same document as query i and j <= i.
All inputs are finite; a program needn't handle non-finite values.
Results may differ from a plain program's by a relative error of at most 0.02.
Values may be sent and summed in bfloat16 or wider, within the bound.
A program may use at most 128 MiB of HBM per device.

v0:
```python
import math

import jax
import jax.numpy as jnp
from jax import lax
from jax.sharding import PartitionSpec as P

DH = 64
NBUCKET = 32
L = 512


NORM_EPSILON = 1e-06
MASKED_SCORE = -1e30
GELU_CUBIC = 0.044715


def to_half(values):
    return values.astype(jnp.bfloat16)


def matmul(left_side, right_side):
    return jnp.dot(left_side, right_side, preferred_element_type=jnp.float32)


def left_contract(left_side, right_side):
    return lax.dot_general(
        left_side, right_side, (((0,), (0,)), ((), ())), preferred_element_type=jnp.float32
    )


def right_contract(left_side, right_side):
    return lax.dot_general(
        left_side, right_side, (((1,), (1,)), ((), ())), preferred_element_type=jnp.float32
    )


def gelu_pair(values):
    root_scale = math.sqrt(2.0 / math.pi)
    interior = root_scale * (values + GELU_CUBIC * values * values * values)
    tangent = jnp.tanh(interior)
    activated = 0.5 * values * (1.0 + tangent)
    slope = 0.5 * (1.0 + tangent) + 0.5 * values * (1.0 - tangent * tangent) * root_scale * (
        1.0 + 3.0 * GELU_CUBIC * values * values
    )
    return (activated, slope)


def norm_forward(stream, gain):
    inverse = lax.rsqrt(jnp.mean(stream * stream, axis=-1, keepdims=True) + NORM_EPSILON)
    unit_rows = stream * inverse
    return (unit_rows, inverse, to_half(unit_rows * gain.astype(jnp.float32)))


def norm_backward(incoming, unit_rows, inverse, gain):
    scaled = incoming * gain.astype(jnp.float32)
    result = inverse * (scaled - unit_rows * jnp.mean(scaled * unit_rows, axis=-1, keepdims=True))
    return (result, jnp.sum(incoming * unit_rows, axis=0))


def spread(rows_local):
    return lax.all_gather(rows_local, "tensor", axis=0, tiled=True)


def collect(partial_rows):
    return lax.psum_scatter(partial_rows, "tensor", scatter_dimension=0, tiled=True)


def bucket_onehot(bucket_rows, position, block_rows):
    indices = lax.dynamic_slice_in_dim(bucket_rows, position * block_rows, block_rows, 0)
    return (indices[None] == lax.iota(jnp.int32, NBUCKET)[:, None, None]).astype(jnp.float32)


def bias_lookup(bucket_rows, position_bias_table):
    block_rows = math.gcd(L, 64)

    def fill_block(position, result):
        bucket_indicator = bucket_onehot(bucket_rows, position, block_rows)
        bias_for_block = jnp.einsum(
            "oat,of->fat", bucket_indicator, position_bias_table, precision=lax.Precision.HIGHEST
        )
        return lax.dynamic_update_slice_in_dim(result, bias_for_block, position * block_rows, 1)

    return lax.fori_loop(
        0, L // block_rows, fill_block, jnp.zeros((position_bias_table.shape[1], L, L), jnp.float32)
    )


def bias_gradient(grad_logits, bucket_rows):
    block_rows = math.gcd(L, 64)

    def add_block(position, summed_totals):
        bucket_indicator = bucket_onehot(bucket_rows, position, block_rows)
        block_logits = lax.dynamic_slice_in_dim(grad_logits, position * block_rows, block_rows, 1)
        return summed_totals + jnp.einsum(
            "ncl,dcl->dn", block_logits, bucket_indicator, precision=lax.Precision.HIGHEST
        )

    return lax.fori_loop(
        0, L // block_rows, add_block, jnp.zeros((NBUCKET, grad_logits.shape[0]), jnp.float32)
    )


def head_split(matrix):
    return matrix.reshape(matrix.shape[0], -1, DH)


def score_matrix(queries, keys, bias, allowed):
    logits = jnp.einsum(
        "qhd,khd->hqk", head_split(queries), head_split(keys), preferred_element_type=jnp.float32
    )
    if bias is not None:
        logits = jnp.where(allowed[None], logits + bias, MASKED_SCORE)
    return logits


def attend(queries, keys, values, bias, allowed):
    logits = score_matrix(queries, keys, bias, allowed)
    row_max = jnp.max(logits, axis=-1, keepdims=True)
    log_total = row_max + jnp.log(jnp.sum(jnp.exp(logits - row_max), axis=-1, keepdims=True))
    probs_half = to_half(jnp.exp(logits - log_total))
    mixed = jnp.einsum(
        "hqk,khd->qhd", probs_half, head_split(values), preferred_element_type=jnp.float32
    )
    return (to_half(mixed.reshape(queries.shape[0], -1)), log_total)


def attend_back(queries, keys, values, bias, allowed, bucket_rows, log_total, grad_mixed):
    logits = score_matrix(queries, keys, bias, allowed)
    probs_full = jnp.exp(logits - log_total)
    grad_values = to_half(
        jnp.einsum(
            "hqk,qhd->khd",
            to_half(probs_full),
            head_split(grad_mixed),
            preferred_element_type=jnp.float32,
        ).reshape(keys.shape[0], -1)
    )
    grad_probs = jnp.einsum(
        "qhd,khd->hqk",
        head_split(grad_mixed),
        head_split(values),
        preferred_element_type=jnp.float32,
    )
    centre = jnp.sum(probs_full * grad_probs, axis=-1, keepdims=True)
    grad_logits = probs_full * (grad_probs - centre)
    logits_half = to_half(grad_logits)
    grad_queries = to_half(
        jnp.einsum(
            "hqk,khd->qhd", logits_half, head_split(keys), preferred_element_type=jnp.float32
        ).reshape(queries.shape[0], -1)
    )
    grad_keys = to_half(
        jnp.einsum(
            "hqk,qhd->khd", logits_half, head_split(queries), preferred_element_type=jnp.float32
        ).reshape(keys.shape[0], -1)
    )
    if bias is not None:
        return (grad_queries, grad_keys, grad_values, bias_gradient(grad_logits, bucket_rows))
    return (grad_queries, grad_keys, grad_values)


def per_device(
    layer_in,
    encoder_states,
    grad_out,
    buckets,
    keep,
    wq_self,
    wk_self,
    wv_self,
    wo_self,
    wq_cross,
    wk_cross,
    wv_cross,
    wo_cross,
    w_gate,
    w_up,
    w_down,
    norm_scales,
    rel_bias,
):
    gathered = (
        lax.all_gather(wq_self, "dp", axis=0, tiled=True),
        lax.all_gather(wk_self, "dp", axis=0, tiled=True),
        lax.all_gather(wv_self, "dp", axis=0, tiled=True),
        lax.all_gather(wo_self, "dp", axis=1, tiled=True),
        lax.all_gather(wq_cross, "dp", axis=0, tiled=True),
        lax.all_gather(wk_cross, "dp", axis=0, tiled=True),
        lax.all_gather(wv_cross, "dp", axis=0, tiled=True),
        lax.all_gather(wo_cross, "dp", axis=1, tiled=True),
        lax.all_gather(w_gate, "dp", axis=0, tiled=True),
        lax.all_gather(w_up, "dp", axis=0, tiled=True),
        lax.all_gather(w_down, "dp", axis=1, tiled=True),
        lax.all_gather(norm_scales, "dp", axis=1, tiled=True),
    )
    (
        self_query,
        self_key,
        self_value,
        self_output,
        cross_query,
        cross_key,
        cross_value,
        cross_output,
        gate_full,
        up_full,
        down_full,
        scales_full,
    ) = gathered
    stream_in = layer_in.astype(jnp.float32)
    unit_one, inverse_one, first_normed_input = norm_forward(stream_in, scales_full[0])
    paired = spread(jnp.stack([first_normed_input, encoder_states], axis=1))
    rows_one = paired[:, 0]
    source_rows = paired[:, 1]
    seq_count = rows_one.shape[0] // L

    def by_sequence(matrix):
        return matrix.reshape(seq_count, L, matrix.shape[-1])

    def joined(matrix):
        return matrix.reshape(seq_count * L, matrix.shape[-1])

    bias_all = lax.map(lambda bucket_rows: bias_lookup(bucket_rows, rel_bias), buckets)
    allowed_all = keep == 1
    self_q = to_half(matmul(rows_one, self_query))
    self_k = to_half(matmul(rows_one, self_key))
    self_v = to_half(matmul(rows_one, self_value))
    mixed_self, total_self = lax.map(
        lambda pieces: attend(pieces[0], pieces[1], pieces[2], pieces[3], pieces[4]),
        (by_sequence(self_q), by_sequence(self_k), by_sequence(self_v), bias_all, allowed_all),
    )
    mixed_self = joined(mixed_self)
    stream_one = stream_in + collect(matmul(mixed_self, self_output))
    unit_two, inverse_two, normed_two = norm_forward(stream_one, scales_full[1])
    rows_two = spread(normed_two)
    cross_q = to_half(matmul(rows_two, cross_query))
    cross_k = to_half(matmul(source_rows, cross_key))
    cross_v = to_half(matmul(source_rows, cross_value))
    mixed_cross, total_cross = lax.map(
        lambda pieces: attend(pieces[0], pieces[1], pieces[2], None, None),
        (by_sequence(cross_q), by_sequence(cross_k), by_sequence(cross_v)),
    )
    mixed_cross = joined(mixed_cross)
    stream_two = stream_one + collect(matmul(mixed_cross, cross_output))
    unit_three, inverse_three, normed_three = norm_forward(stream_two, scales_full[2])
    rows_three = spread(normed_three)
    gate_rows = matmul(rows_three, gate_full)
    up_rows = matmul(rows_three, up_full)
    activated, slope = gelu_pair(gate_rows)
    hidden = to_half(activated * up_rows)
    layer_out = to_half(stream_two + collect(matmul(hidden, down_full)))
    (
        back_sq,
        back_sk,
        back_sv,
        back_so,
        back_cq,
        cross_key_backward,
        back_cv,
        back_co,
        back_gate,
        back_up,
        back_down,
        back_scales,
    ) = gathered
    grad_rows = spread(grad_out)
    grad_hidden = right_contract(grad_rows, back_down)
    grad_w_down = left_contract(hidden, grad_rows)
    grad_gate = to_half(grad_hidden * up_rows * slope)
    grad_up = to_half(grad_hidden * activated)
    grad_w_gate = left_contract(rows_three, grad_gate)
    grad_w_up = left_contract(rows_three, grad_up)
    grad_normed_three = collect(
        right_contract(grad_gate, back_gate) + right_contract(grad_up, back_up)
    )
    back_three, gain_three = norm_backward(
        grad_normed_three, unit_three, inverse_three, back_scales[2]
    )
    grad_stream_two = grad_out.astype(jnp.float32) + back_three
    grad_two_rows = spread(to_half(grad_stream_two))
    grad_mixed_cross = to_half(right_contract(grad_two_rows, back_co))
    grad_wo_cross = left_contract(mixed_cross, grad_two_rows)
    grad_q_cross, cross_key_gradient, grad_v_cross = lax.map(
        lambda pieces: attend_back(
            pieces[0], pieces[1], pieces[2], None, None, None, pieces[3], pieces[4]
        ),
        (
            by_sequence(cross_q),
            by_sequence(cross_k),
            by_sequence(cross_v),
            total_cross,
            by_sequence(grad_mixed_cross),
        ),
    )
    grad_q_cross = joined(grad_q_cross)
    cross_key_gradient = joined(cross_key_gradient)
    grad_v_cross = joined(grad_v_cross)
    grad_wq_cross = left_contract(rows_two, grad_q_cross)
    grad_wk_cross = left_contract(source_rows, cross_key_gradient)
    grad_wv_cross = left_contract(source_rows, grad_v_cross)
    cross_pair = collect(
        jnp.stack(
            [
                right_contract(grad_q_cross, back_cq),
                right_contract(cross_key_gradient, cross_key_backward)
                + right_contract(grad_v_cross, back_cv),
            ],
            axis=1,
        )
    )
    grad_encoder = cross_pair[:, 1]
    back_two, gain_two = norm_backward(cross_pair[:, 0], unit_two, inverse_two, back_scales[1])
    grad_stream_one = grad_stream_two + back_two
    grad_one_rows = spread(to_half(grad_stream_one))
    grad_mixed_self = to_half(right_contract(grad_one_rows, back_so))
    grad_wo_self = left_contract(mixed_self, grad_one_rows)
    grad_q_self, grad_k_self, grad_v_self, bias_parts = lax.map(
        lambda pieces: attend_back(
            pieces[0], pieces[1], pieces[2], pieces[3], pieces[4], pieces[5], pieces[6], pieces[7]
        ),
        (
            by_sequence(self_q),
            by_sequence(self_k),
            by_sequence(self_v),
            bias_all,
            allowed_all,
            buckets,
            total_self,
            by_sequence(grad_mixed_self),
        ),
    )
    grad_q_self = joined(grad_q_self)
    grad_k_self = joined(grad_k_self)
    grad_v_self = joined(grad_v_self)
    grad_wq_self = left_contract(rows_one, grad_q_self)
    grad_wk_self = left_contract(rows_one, grad_k_self)
    grad_wv_self = left_contract(rows_one, grad_v_self)
    grad_normed_one = collect(
        right_contract(grad_q_self, back_sq)
        + right_contract(grad_k_self, back_sk)
        + right_contract(grad_v_self, back_sv)
    )
    back_one, gain_one = norm_backward(grad_normed_one, unit_one, inverse_one, back_scales[0])
    grad_in = grad_stream_one + back_one
    summed = (
        lax.psum_scatter(grad_wq_self, "dp", scatter_dimension=0, tiled=True),
        lax.psum_scatter(grad_wk_self, "dp", scatter_dimension=0, tiled=True),
        lax.psum_scatter(grad_wv_self, "dp", scatter_dimension=0, tiled=True),
        lax.psum_scatter(grad_wo_self, "dp", scatter_dimension=1, tiled=True),
        lax.psum_scatter(grad_wq_cross, "dp", scatter_dimension=0, tiled=True),
        lax.psum_scatter(grad_wk_cross, "dp", scatter_dimension=0, tiled=True),
        lax.psum_scatter(grad_wv_cross, "dp", scatter_dimension=0, tiled=True),
        lax.psum_scatter(grad_wo_cross, "dp", scatter_dimension=1, tiled=True),
        lax.psum_scatter(grad_w_gate, "dp", scatter_dimension=0, tiled=True),
        lax.psum_scatter(grad_w_up, "dp", scatter_dimension=0, tiled=True),
        lax.psum_scatter(grad_w_down, "dp", scatter_dimension=1, tiled=True),
    )
    grad_norm_scales = lax.psum_scatter(
        jnp.stack([gain_one, gain_two, gain_three]),
        ("dp", "tensor"),
        scatter_dimension=1,
        tiled=True,
    )
    grad_rel_bias = lax.psum(jnp.sum(bias_parts, axis=0), "dp")
    return (
        layer_out,
        grad_in,
        grad_encoder,
        summed[0],
        summed[1],
        summed[2],
        summed[3],
        summed[4],
        summed[5],
        summed[6],
        summed[7],
        summed[8],
        summed[9],
        summed[10],
        grad_norm_scales,
        grad_rel_bias,
    )


def solution(mesh):
    in_specs = (
        P(("dp", "tensor"), None),
        P(("dp", "tensor"), None),
        P(("dp", "tensor"), None),
        P("dp", None, None),
        P("dp", None, None),
        P("dp", "tensor"),
        P("dp", "tensor"),
        P("dp", "tensor"),
        P("tensor", "dp"),
        P("dp", "tensor"),
        P("dp", "tensor"),
        P("dp", "tensor"),
        P("tensor", "dp"),
        P("dp", "tensor"),
        P("dp", "tensor"),
        P("tensor", "dp"),
        P(None, "dp"),
        P(None, "tensor"),
    )
    out_specs = (
        P(("dp", "tensor"), None),
        P(("dp", "tensor"), None),
        P(("dp", "tensor"), None),
        P("dp", "tensor"),
        P("dp", "tensor"),
        P("dp", "tensor"),
        P("tensor", "dp"),
        P("dp", "tensor"),
        P("dp", "tensor"),
        P("dp", "tensor"),
        P("tensor", "dp"),
        P("dp", "tensor"),
        P("dp", "tensor"),
        P("tensor", "dp"),
        P(None, ("dp", "tensor")),
        P(None, "tensor"),
    )
    return jax.shard_map(
        per_device, mesh=mesh, in_specs=in_specs, out_specs=out_specs, check_vma=False
    )
```

profile of v0, /device:TPU:13, one launch (start us, length us, event | category | flops | bytes accessed | tf_op | source)
XLA Modules:
  0.0 1371.7 jit_solution(16480803349521607683)
XLA Ops:
  108.3 25.1 %all_gather.58 = bf16[768,192]{1,0:T(8,128)(2,1)S(1)} all-gather(bf16[96,192]{1,0:T(8,128)(2,1)S(1)} %copy-done.66), channel_id=1, replica_groups=mesh['dp'=8,'tensor'=4] {'dp'}, dimensions={0}, use_global_device_ids=true | all-gather | bytes 331776 | tf_op jit(solution)/shard_map/all_gather | solution.py:185
  133.4 27.3 %all_gather.56 = bf16[768,192]{1,0:T(8,128)(2,1)} all-gather(bf16[96,192]{1,0:T(8,128)(2,1)S(1)} %copy-done.67), channel_id=1, replica_groups=mesh['dp'=8,'tensor'=4] {'dp'}, dimensions={0}, use_global_device_ids=true | all-gather | bytes 331776 | tf_op jit(solution)/shard_map/all_gather | solution.py:186
  173.2 27.7 %all_gather.64 = bf16[192,768]{0,1:T(8,128)(2,1)} all-gather(bf16[192,96]{0,1:T(8,128)(2,1)S(1)} %copy.63), channel_id=1, replica_groups=mesh['dp'=8,'tensor'=4] {'dp'}, dimensions={1}, use_global_device_ids=true | all-gather | bytes 331776 | tf_op jit(solution)/shard_map/all_gather | solution.py:191
  200.9 27.6 %all_gather.62 = bf16[768,192]{1,0:T(8,128)(2,1)} all-gather(bf16[96,192]{1,0:T(8,128)(2,1)} %param.31), channel_id=1, replica_groups=mesh['dp'=8,'tensor'=4] {'dp'}, dimensions={0}, use_global_device_ids=true | all-gather | bytes 331776 | tf_op jit(solution)/shard_map/all_gather | solution.py:188
  253.6 26.6 %all_gather.60 = bf16[768,192]{1,0:T(8,128)(2,1)S(1)} all-gather(bf16[96,192]{1,0:T(8,128)(2,1)} %param.33), channel_id=1, replica_groups=mesh['dp'=8,'tensor'=4] {'dp'}, dimensions={0}, use_global_device_ids=true | all-gather | bytes 331776 | tf_op jit(solution)/shard_map/all_gather | solution.py:190
  285.5 58.9 %all_gather.61 = bf16[512,768]{1,0:T(8,128)(2,1)S(1)} all-gather(bf16[128,768]{1,0:T(8,128)(2,1)S(1)} %multiply_convert_fusion.4), channel_id=1, replica_groups=mesh['dp'=8,'tensor'=4] {'tensor'}, dimensions={0}, use_global_device_ids=true | all-gather | bytes 983040 | tf_op jit(solution)/shard_map/all_gather | solution.py:62
  360.4 28.8 %all_gather.66 = bf16[768,512]{1,0:T(8,128)(2,1)} all-gather(bf16[96,512]{1,0:T(8,128)(2,1)} %param.35), channel_id=1, replica_groups=mesh['dp'=8,'tensor'=4] {'dp'}, dimensions={0}, use_global_device_ids=true | all-gather | bytes 884736 | tf_op jit(solution)/shard_map/all_gather | solution.py:192
  389.3 29.4 %all_gather.67 = bf16[768,512]{1,0:T(8,128)(2,1)} all-gather(bf16[96,512]{1,0:T(8,128)(2,1)} %param.36), channel_id=1, replica_groups=mesh['dp'=8,'tensor'=4] {'dp'}, dimensions={0}, use_global_device_ids=true | all-gather | bytes 884736 | tf_op jit(solution)/shard_map/all_gather | solution.py:193
  418.7 28.5 %all_gather.68 = bf16[512,768]{0,1:T(8,128)(2,1)} all-gather(bf16[512,96]{0,1:T(8,128)(2,1)} %param.37), channel_id=1, replica_groups=mesh['dp'=8,'tensor'=4] {'dp'}, dimensions={1}, use_global_device_ids=true | all-gather | bytes 884736 | tf_op jit(solution)/shard_map/all_gather | solution.py:194
  449.9 25.4 %all_gather.65 = bf16[512,768]{1,0:T(8,128)(2,1)S(1)} all-gather(bf16[128,768]{1,0:T(8,128)(2,1)S(1)} %multiply_convert_fusion.3), channel_id=1, replica_groups=mesh['dp'=8,'tensor'=4] {'tensor'}, dimensions={0}, use_global_device_ids=true | all-gather | bytes 983040 | tf_op jit(solution)/shard_map/all_gather | solution.py:62
  483.3 30.6 %reduce-scatter.29.cloned.1.call-done = f32[128,768]{1,0:T(8,128)} async-done(((f32[512,768]{1,0:T(8,128)}), f32[128,768]{1,0:T(8,128)}) %reduce-scatter.29.cloned.1.call-update) | async-done | bytes 393232 | tf_op jit(solution)/shard_map/reduce_scatter | solution.py:66
  540.9 32.0 %reduce-scatter.31.cloned.1.call-done = f32[128,2,768]{2,0,1:T(8,128)} async-done(((f32[512,2,768]{2,0,1:T(8,128)}), f32[128,2,768]{2,0,1:T(8,128)}) %reduce-scatter.31.cloned.1.call-update) | async-done | bytes 786448 | tf_op jit(solution)/shard_map/reduce_scatter | solution.py:66
  575.3 28.1 %reduce-scatter.27.cloned.1.call-done = f32[128,768]{1,0:T(8,128)} async-done(((f32[512,768]{1,0:T(8,128)}), f32[128,768]{1,0:T(8,128)}) %reduce-scatter.27.cloned.1.call-update) | async-done | bytes 393232 | tf_op jit(solution)/shard_map/reduce_scatter | solution.py:66
  675.2 33.7 %while.29 = (s32[]{:T(128)}, f32[32,3]{0,1:T(4,128)S(1)}, s32[512,512]{1,0:T(8,128)}, f32[3,512,512]{2,0,1:T(4,128)}, s32[]{:T(128)}, /*index=5*/s32[]{:T(128)}, s32[]{:T(128)}, s32[]{:T(128)}) while((s32[]{:T(128)}, f32[32,3]{0,1:T(4,128)S(1)}, s32[512,512]{1,0:T(8,128)}, f32[3,512,512]{2,0,1:T(4,128)}, s32[]{:T(128)}, ...), condition=%wide.region_36.37_spmd.clone, body=%wide.region_35.36_spmd.clone.sunk | while | flops 38797512 | bytes 918429 | solution.py:99
  735.3 29.8 %reduce-scatter.33.cloned.1.call-done = f32[128,768]{1,0:T(8,128)} async-done(((f32[512,768]{1,0:T(8,128)}), f32[128,768]{1,0:T(8,128)}) %reduce-scatter.33.cloned.1.call-update) | async-done | bytes 393232 | tf_op jit(solution)/shard_map/reduce_scatter | solution.py:66
  766.4 40.0 %all-reduce = f32[3,768]{1,0:T(4,128)S(1)} all-reduce(f32[3,768]{1,0:T(4,128)S(1)} %pad_maximum_fusion.2), channel_id=19, replica_groups=mesh['dp'=8,'tensor'=4] {'dp','tensor'}, use_global_device_ids=true, to_apply=%region_34.35.clone | all-reduce | flops 2304 | bytes 18432
  832.6 68.4 %reduce-scatter.49.cloned.1.call-done = f32[96,512]{1,0:T(8,128)} async-done(((f32[768,512]{1,0:T(8,128)}), f32[96,512]{1,0:T(8,128)}) %reduce-scatter.49.cloned.1.call-update) | async-done | bytes 196624 | tf_op jit(solution)/shard_map/reduce_scatter | solution.py:356
  901.0 68.2 %reduce-scatter.47.cloned.1.call-done = f32[96,512]{1,0:T(8,128)} async-done(((f32[768,512]{1,0:T(8,128)}), f32[96,512]{1,0:T(8,128)}) %reduce-scatter.47.cloned.1.call-update) | async-done | bytes 196624 | tf_op jit(solution)/shard_map/reduce_scatter | solution.py:355
  969.2 66.4 %reduce-scatter.45.cloned.1.call-done = f32[96,192]{1,0:T(8,128)} async-done(((f32[768,192]{1,0:T(8,128)}), f32[96,192]{1,0:T(8,128)}) %reduce-scatter.45.cloned.1.call-update) | async-done | bytes 73744 | tf_op jit(solution)/shard_map/reduce_scatter | solution.py:353
  1035.6 65.5 %reduce-scatter.41.cloned.1.call-done = f32[96,192]{1,0:T(8,128)} async-done(((f32[768,192]{1,0:T(8,128)}), f32[96,192]{1,0:T(8,128)}) %reduce-scatter.41.cloned.1.call-update) | async-done | bytes 73744 | tf_op jit(solution)/shard_map/reduce_scatter | solution.py:351
  1101.1 66.0 %reduce-scatter.43.cloned.1.call-done = f32[96,192]{1,0:T(8,128)} async-done(((f32[768,192]{1,0:T(8,128)}), f32[96,192]{1,0:T(8,128)}) %reduce-scatter.43.cloned.1.call-update) | async-done | bytes 73744 | tf_op jit(solution)/shard_map/reduce_scatter | solution.py:352
  1167.0 66.0 %reduce-scatter.39.cloned.1.call-done = f32[96,192]{1,0:T(8,128)} async-done(((f32[768,192]{1,0:T(8,128)}), f32[96,192]{1,0:T(8,128)}) %reduce-scatter.39.cloned.1.call-update) | async-done | bytes 73744 | tf_op jit(solution)/shard_map/reduce_scatter | solution.py:349
  1233.0 65.9 %reduce-scatter.37.cloned.1.call-done = f32[96,192]{1,0:T(8,128)} async-done(((f32[768,192]{1,0:T(8,128)}), f32[96,192]{1,0:T(8,128)}) %reduce-scatter.37.cloned.1.call-update) | async-done | bytes 73744 | tf_op jit(solution)/shard_map/reduce_scatter | solution.py:348
  1298.9 65.9 %reduce-scatter.35.cloned.1.call-done = f32[96,192]{1,0:T(8,128)} async-done(((f32[768,192]{1,0:T(8,128)}), f32[96,192]{1,0:T(8,128)}) %reduce-scatter.35.cloned.1.call-update) | async-done | bytes 73744 | tf_op jit(solution)/shard_map/reduce_scatter | solution.py:347
  (325 shorter events, 382.7 us)
Async XLA Ops:
  7.2 153.6 %all-gather.3.cloned.1.call-start = ((), (), s32[]{:S(2)}) async-start(), calls=%async_computation.17 | async-start | bytes 1966080 | tf_op jit(solution)/shard_map/all_gather | solution.py:62
  20.0 265.0 %copy-start.63 = (f32[768]{0:T(1024)}, f32[768]{0:T(1024)S(1)}, u32[]{:S(2)}) copy-start(f32[768]{0:T(1024)S(1)} %get-tuple-element.342) | copy-start | bytes 9220
  23.4 260.3 %reduce-scatter.23.cloned.1.call-start = ((), (), s32[]{:S(2)}) async-start(), calls=%async_computation.18 | async-start | bytes 1966080 | tf_op jit(solution)/shard_map/reduce_scatter | solution.py:66
  172.2 274.9 %reduce-scatter.25.cloned.1.call-start = ((), (), s32[]{:S(2)}) async-start(), calls=%async_computation.19 | async-start | bytes 1966080 | tf_op jit(solution)/shard_map/reduce_scatter | solution.py:66
  173.2 109.4 %copy-start.7 = (bf16[512,2,768]{2,0,1:T(8,128)(2,1)S(1)}, bf16[512,2,768]{2,0,1:T(8,128)(2,1)}, u32[]{:S(2)}) copy-start(bf16[512,2,768]{2,0,1:T(8,128)(2,1)} %all-gather.3.cloned.1.call-done) | copy-start | bytes 4718596
  350.7 163.2 %reduce-scatter.29.cloned.1.call-start = ((), (), s32[]{:S(2)}) async-start(), calls=%async_computation.21 | async-start | bytes 1966080 | tf_op jit(solution)/shard_map/reduce_scatter | solution.py:66
  483.3 89.7 %reduce-scatter.31.cloned.1.call-start = ((), (), s32[]{:S(2)}) async-start(), calls=%async_computation.22 | async-start | bytes 3932160 | tf_op jit(solution)/shard_map/reduce_scatter | solution.py:66
  535.1 68.3 %reduce-scatter.27.cloned.1.call-start = ((), (), s32[]{:S(2)}) async-start(), calls=%async_computation.20 | async-start | bytes 1966080 | tf_op jit(solution)/shard_map/reduce_scatter | solution.py:66
  538.2 129.4 %reduce-scatter.55.cloned.1.call-start = ((), (), s32[]{:S(2)}) async-start(), calls=%async_computation.34 | async-start | bytes 884736
  540.9 192.8 %reduce-scatter.53.cloned.1.call-start = ((), (), s32[]{:S(2)}) async-start(), calls=%async_computation.33 | async-start | bytes 884736
  623.8 141.3 %reduce-scatter.33.cloned.1.call-start = ((), (), s32[]{:S(2)}) async-start(), calls=%async_computation.23 | async-start | bytes 1966080 | tf_op jit(solution)/shard_map/reduce_scatter | solution.py:66
  629.8 202.8 %reduce-scatter.51.cloned.1.call-start = ((), (), s32[]{:S(2)}) async-start(), calls=%async_computation.32 | async-start | bytes 1769472 | tf_op jit(solution)/shard_map/reduce_scatter | solution.py:357
  631.7 269.3 %reduce-scatter.49.cloned.1.call-start = ((), (), s32[]{:S(2)}) async-start(), calls=%async_computation.31 | async-start | bytes 1769472 | tf_op jit(solution)/shard_map/reduce_scatter | solution.py:356
  633.5 335.7 %reduce-scatter.47.cloned.1.call-start = ((), (), s32[]{:S(2)}) async-start(), calls=%async_computation.30 | async-start | bytes 1769472 | tf_op jit(solution)/shard_map/reduce_scatter | solution.py:355
  636.6 399.0 %reduce-scatter.45.cloned.1.call-start = ((), (), s32[]{:S(2)}) async-start(), calls=%async_computation.29 | async-start | bytes 884736 | tf_op jit(solution)/shard_map/reduce_scatter | solution.py:353
  638.0 463.1 %reduce-scatter.41.cloned.1.call-start = ((), (), s32[]{:S(2)}) async-start(), calls=%async_computation.27 | async-start | bytes 884736 | tf_op jit(solution)/shard_map/reduce_scatter | solution.py:351
  639.4 527.6 %reduce-scatter.43.cloned.1.call-start = ((), (), s32[]{:S(2)}) async-start(), calls=%async_computation.28 | async-start | bytes 884736 | tf_op jit(solution)/shard_map/reduce_scatter | solution.py:352
  640.8 592.1 %reduce-scatter.39.cloned.1.call-start = ((), (), s32[]{:S(2)}) async-start(), calls=%async_computation.26 | async-start | bytes 884736 | tf_op jit(solution)/shard_map/reduce_scatter | solution.py:349
  643.5 655.4 %reduce-scatter.37.cloned.1.call-start = ((), (), s32[]{:S(2)}) async-start(), calls=%async_computation.25 | async-start | bytes 884736 | tf_op jit(solution)/shard_map/reduce_scatter | solution.py:348
  646.1 718.7 %reduce-scatter.35.cloned.1.call-start = ((), (), s32[]{:S(2)}) async-start(), calls=%async_computation.24 | async-start | bytes 884736 | tf_op jit(solution)/shard_map/reduce_scatter | solution.py:347
  675.2 89.9 %copy-start.15 = (bf16[128,768]{1,0:T(8,128)(2,1)S(1)}, bf16[128,768]{1,0:T(8,128)(2,1)}, u32[]{:S(2)}) copy-start(bf16[128,768]{1,0:T(8,128)(2,1)} %param.22) | copy-start | bytes 589828
  675.2 89.9 %copy-start.62 = (f32[768]{0:T(1024)S(1)}, f32[768]{0:T(1024)}, u32[]{:S(2)}) copy-start(f32[768]{0:T(1024)} %copy-done.61) | copy-start | bytes 9220
  675.2 89.9 %copy-start.72 = (f32[128]{0:T(128)S(1)}, f32[128]{0:T(128)}, u32[]{:S(2)}) copy-start(f32[128]{0:T(128)} %copy-done.71) | copy-start | bytes 1540
  675.2 131.8 %copy-start.41 = (f32[128,768]{1,0:T(8,128)S(1)}, f32[128,768]{1,0:T(8,128)}, u32[]{:S(2)}) copy-start(f32[128,768]{1,0:T(8,128)} %get-tuple-element.361) | copy-start | bytes 1179652
  (70 other events, 881.5 us)
Sparse Core Ops, SparseCore 0:
  23.5 27.1 all-gather.2
  172.4 59.6 reduce-scatter.22
  350.8 30.2 reduce-scatter.24
  483.4 30.4 reduce-scatter.28
  535.2 37.7 reduce-scatter.30
  575.3 28.0 reduce-scatter.26
  606.7 60.8 reduce-scatter.54
  670.9 62.6 reduce-scatter.52
  736.2 28.8 reduce-scatter.32
  769.0 63.6 reduce-scatter.50
  836.6 64.3 reduce-scatter.48
  904.9 64.2 reduce-scatter.46
  973.1 62.4 reduce-scatter.44
  1039.3 61.7 reduce-scatter.40
  1104.8 62.1 reduce-scatter.42
  1170.8 62.1 reduce-scatter.38
  1236.7 62.1 reduce-scatter.36
  1302.6 62.1 reduce-scatter.34
where the time goes:
time: 1380 us; the launch traced here: 1370 us
  waiting for transfers between devices  710 us (51%)
  blocking collectives  471 us (34%)
  matrix products  107 us (8%)
  local copies, waits for them, and re-layouts  41.4 us (3%)
  other arithmetic  26.9 us (2%)
  between operations  15.2 us (1%)
    reduce_scatter x6, waiting for transfers between devices, collect(): lax.psum_scatter(partial_rows, 'tensor', scatter_dimension=0, tiled=True)  121 us
    all_gather x5, blocking collectives, spread(): return lax.all_gather(rows_local, 'tensor', axis=0, tiled=True)  112 us
    reduce_scatter x1, waiting for transfers between devices, per_device(): lax.psum_scatter(grad_w_up, 'dp', scatter_dimension=0, tiled=True)  68.4 us
    reduce_scatter x1, waiting for transfers between devices, per_device(): lax.psum_scatter(grad_w_gate, 'dp', scatter_dimension=0, tiled=True)  68.2 us
    reduce_scatter x1, waiting for transfers between devices, per_device(): lax.psum_scatter(grad_wv_cross, 'dp', scatter_dimension=0, tiled=True)  66.4 us
    reduce_scatter x1, waiting for transfers between devices, per_device(): lax.psum_scatter(grad_wv_self, 'dp', scatter_dimension=0, tiled=True)  66 us
    reduce_scatter x1, waiting for transfers between devices, per_device(): lax.psum_scatter(grad_wk_cross, 'dp', scatter_dimension=0, tiled=True)  66 us
    reduce_scatter x1, waiting for transfers between devices, per_device(): lax.psum_scatter(grad_wq_self, 'dp', scatter_dimension=0, tiled=True)  65.9 us
  transfers between devices with their start and end apart: 18, of which 15 were waited for; matrix products, arithmetic and copies ran while one was open for 9% of the time, Pallas kernels for 0%

commit v1 on v0

v1 whole, which is shorter than its diff:
```python
import math

import jax
import jax.numpy as jnp
import numpy as np
from jax import lax
from jax.experimental import pallas as pl
from jax.experimental.pallas import tpu as pltpu
from jax.sharding import PartitionSpec as P

DH = 64
NBUCKET = 32
L = 512
BLOCK = 128
NORM_EPSILON = 1e-06
MASKED_SCORE = -1e30
GELU_CUBIC = 0.044715
F32 = jnp.float32
BF16 = jnp.bfloat16


def to_half(values):
    return values.astype(BF16)


def matmul(left_side, right_side):
    return jnp.dot(left_side, right_side, preferred_element_type=F32)


def left_contract(left_side, right_side):
    return lax.dot_general(left_side, right_side, (((0,), (0,)), ((), ())), preferred_element_type=F32)


def right_contract(left_side, right_side):
    return lax.dot_general(left_side, right_side, (((1,), (1,)), ((), ())), preferred_element_type=F32)


def gelu_pair(values):
    root_scale = math.sqrt(2.0 / math.pi)
    interior = root_scale * (values + GELU_CUBIC * values * values * values)
    tangent = jnp.tanh(interior)
    activated = 0.5 * values * (1.0 + tangent)
    slope = 0.5 * (1.0 + tangent) + 0.5 * values * (1.0 - tangent * tangent) * root_scale * (
        1.0 + 3.0 * GELU_CUBIC * values * values
    )
    return (activated, slope)


def unit_norm(stream):
    inverse = lax.rsqrt(jnp.mean(stream * stream, axis=-1, keepdims=True) + NORM_EPSILON)
    return (stream * inverse, inverse)


def norm_backward(incoming, unit_rows, inverse, gain):
    scaled = incoming * gain
    result = inverse * (scaled - unit_rows * jnp.mean(scaled * unit_rows, axis=-1, keepdims=True))
    return (result, jnp.sum(incoming * unit_rows, axis=0))


def spread(rows_local):
    return lax.all_gather(rows_local, "tensor", axis=0, tiled=True)


def collect(partial_rows):
    return lax.psum_scatter(to_half(partial_rows), "tensor", scatter_dimension=0, tiled=True).astype(F32)


def distance_indicator():
    exact = NBUCKET // 2
    distance = (-np.arange(L)) % L
    log_part = exact + np.floor(
        np.log(np.maximum(distance, 1) / exact) / np.log(128 / exact) * (NBUCKET - exact)
    ).astype(np.int64)
    bucket = np.where(distance < exact, distance, np.minimum(log_part, NBUCKET - 1))
    return (bucket[None, :] == np.arange(NBUCKET)[:, None]).astype(np.float32)


def whole(*shape_and_type):
    return jax.ShapeDtypeStruct(*shape_and_type)


def call(kernel, outs, scratch=(), name=None):
    return pl.pallas_call(
        kernel,
        out_shape=outs,
        scratch_shapes=list(scratch),
        name=name,
        compiler_params=pltpu.CompilerParams(vmem_limit_bytes=60 * 1024 * 1024),
    )


def attend_block(q, k, v, bias, allowed):
    logits = right_contract(q, k)
    if bias is not None:
        logits = jnp.where(allowed, logits + bias, MASKED_SCORE)
    row_max = jnp.max(logits, axis=-1, keepdims=True)
    powers = jnp.exp(logits - row_max)
    probs = to_half(powers / jnp.sum(powers, axis=-1, keepdims=True))
    return probs, to_half(matmul(probs, v))


def attend_kernel(masked, qkv_ref, *refs):
    if masked:
        base_ref, keep_ref, mixed_ref, probs_ref = refs
    else:
        mixed_ref, probs_ref = refs
    width = mixed_ref.shape[1]
    heads = width // DH
    for block in range(L // BLOCK):
        rows = slice(block * BLOCK, (block + 1) * BLOCK)
        reach = (block + 1) * BLOCK if masked else L
        allowed = keep_ref[rows, :reach] == 1 if masked else None
        pieces = []
        for h in range(heads):
            bias = None
            if masked:
                base = base_ref[h]
                tiles = [
                    pltpu.roll(base, 8 * t, 1) if t else base
                    for t in range(block * BLOCK // 8, (block + 1) * BLOCK // 8)
                ]
                bias = jnp.concatenate(tiles, axis=0)[:, :reach]
            probs, mixed = attend_block(
                qkv_ref[rows, h * DH:(h + 1) * DH],
                qkv_ref[:reach, width + h * DH:width + (h + 1) * DH],
                qkv_ref[:reach, 2 * width + h * DH:2 * width + (h + 1) * DH],
                bias,
                allowed,
            )
            probs_ref[h, rows, :reach] = probs
            pieces.append(mixed)
        mixed_ref[rows, :] = jnp.concatenate(pieces, axis=1)


def attend_back_kernel(masked, qkv_ref, probs_ref, gm_ref, grad_ref, *refs):
    if masked:
        diag_ref, key_total, value_total = refs
    else:
        key_total, value_total = refs
    width = gm_ref.shape[1]
    heads = width // DH
    for h in range(heads):
        cq = slice(h * DH, (h + 1) * DH)
        ck = slice(width + h * DH, width + (h + 1) * DH)
        cv = slice(2 * width + h * DH, 2 * width + (h + 1) * DH)
        diag = jnp.zeros((8, L), F32)
        for block in reversed(range(L // BLOCK)):
            rows = slice(block * BLOCK, (block + 1) * BLOCK)
            reach = (block + 1) * BLOCK if masked else L
            probs = probs_ref[h, rows, :reach]
            gm = gm_ref[rows, cq]
            grad_probs = right_contract(gm, qkv_ref[:reach, cv])
            probs_full = probs.astype(F32)
            centre = jnp.sum(probs_full * grad_probs, axis=-1, keepdims=True)
            grad_logits = probs_full * (grad_probs - centre)
            half = to_half(grad_logits)
            grad_ref[rows, cq] = to_half(matmul(half, qkv_ref[:reach, ck]))
            key_part = left_contract(half, qkv_ref[rows, cq])
            value_part = left_contract(probs, gm)
            if block == L // BLOCK - 1:
                key_total[:, :] = key_part
                value_total[:, :] = value_part
            else:
                key_total[:reach, :] += key_part
                value_total[:reach, :] += value_part
            if masked:
                for t in range(BLOCK // 8):
                    tile = grad_logits[8 * t:8 * t + 8]
                    if reach < L:
                        tile = jnp.concatenate([tile, jnp.zeros((8, L - reach), F32)], axis=1)
                    shift = (L - (block * BLOCK + 8 * t)) % L
                    diag = diag + (pltpu.roll(tile, shift, 1) if shift else tile)
        grad_ref[:, ck] = to_half(key_total[...])
        grad_ref[:, cv] = to_half(value_total[...])
        if masked:
            total = diag[0:1]
            for s in range(1, 8):
                total = total + pltpu.roll(diag[s:s + 1], L - s, 1)
            diag_ref[h:h + 1, :] = total


def attend(qkv, base, keep):
    width = qkv.shape[1] // 3
    outs = (
        whole((L, width), BF16),
        whole((width // DH, L, L), BF16),
    )
    if base is None:
        return call(lambda *r: attend_kernel(False, *r), outs, name="cross_fwd")(qkv)
    return call(lambda *r: attend_kernel(True, *r), outs, name="self_fwd")(qkv, base, keep)


def attend_back(qkv, probs, grad_mixed, masked):
    width = qkv.shape[1] // 3
    scratch = (pltpu.VMEM((L, DH), F32), pltpu.VMEM((L, DH), F32))
    grads = whole((L, 3 * width), BF16)
    if masked:
        return call(
            lambda *r: attend_back_kernel(True, *r),
            (grads, whole((width // DH, L), F32)),
            scratch,
            name="self_bwd",
        )(qkv, probs, grad_mixed)
    return call(lambda *r: attend_back_kernel(False, *r), grads, scratch, name="cross_bwd")(
        qkv, probs, grad_mixed
    )


def gather_weights(*parts):
    return lax.all_gather(jnp.concatenate(parts, axis=1), "dp", axis=0, tiled=True)


def scatter_grads(*parts):
    return lax.psum_scatter(to_half(jnp.concatenate(parts, axis=1)), "dp", scatter_dimension=0, tiled=True).astype(F32)


def per_device(
    layer_in,
    encoder_states,
    grad_out,
    buckets,
    keep,
    wq_self,
    wk_self,
    wv_self,
    wo_self,
    wq_cross,
    wk_cross,
    wv_cross,
    wo_cross,
    w_gate,
    w_up,
    w_down,
    norm_scales,
    rel_bias,
):
    W = wq_self.shape[1]
    FFL = w_gate.shape[1]
    D = layer_in.shape[1]
    RL = layer_in.shape[0]
    heads = W // DH
    t_index = lax.axis_index("tensor")
    indicator = jnp.asarray(distance_indicator())
    base_row = jnp.einsum("bm,bh->hm", indicator, rel_bias, precision=lax.Precision.HIGHEST)
    base = jnp.stack([jnp.roll(base_row, s, axis=1) for s in range(8)], axis=1)

    first = gather_weights(wq_self, wk_self, wv_self, norm_scales.T)
    rows_all = spread(jnp.concatenate([layer_in, encoder_states, grad_out], axis=1))
    second = gather_weights(wo_self.T, wq_cross, wk_cross, wv_cross, wo_cross.T)
    third = gather_weights(w_gate, w_up, w_down.T)
    self_qkv_w = first[:, :3 * W]
    gains = first[:, 3 * W:].T.astype(F32)
    self_out_t = second[:, :W]
    cross_q_w = second[:, W:2 * W]
    cross_kv_w = second[:, 2 * W:4 * W]
    cross_out_t = second[:, 4 * W:]
    gate_up_w = third[:, :2 * FFL]
    down_t = third[:, 2 * FFL:]

    stream_all = rows_all[:, :D]
    source_rows = rows_all[:, D:2 * D]
    grad_rows = rows_all[:, 2 * D:]
    rows_one = to_half(unit_norm(stream_all.astype(F32))[0] * gains[0:1])
    stream_in = layer_in.astype(F32)
    unit_one, inverse_one = unit_norm(stream_in)

    self_qkv = to_half(matmul(rows_one, self_qkv_w))
    mixed_self, probs_self = attend(self_qkv, base, keep[0])
    stream_one = stream_in + collect(right_contract(mixed_self, self_out_t))
    unit_two, inverse_two = unit_norm(stream_one)
    rows_two = spread(to_half(unit_two * gains[1:2]))
    cross_qkv = jnp.concatenate(
        [to_half(matmul(rows_two, cross_q_w)), to_half(matmul(source_rows, cross_kv_w))], axis=1
    )
    mixed_cross, probs_cross = attend(cross_qkv, None, None)
    stream_two = stream_one + collect(right_contract(mixed_cross, cross_out_t))
    unit_three, inverse_three = unit_norm(stream_two)
    rows_three = spread(to_half(unit_three * gains[2:3]))
    gate_up = matmul(rows_three, gate_up_w)
    up_rows = gate_up[:, FFL:]
    activated, slope = gelu_pair(gate_up[:, :FFL])
    hidden = to_half(activated * up_rows)
    grad_hidden = matmul(grad_rows, down_t)
    grad_gate_up = to_half(
        jnp.concatenate([grad_hidden * up_rows * slope, grad_hidden * activated], axis=1)
    )
    grad_normed_three = collect(right_contract(grad_gate_up, gate_up_w))
    layer_out = to_half(stream_two + collect(right_contract(hidden, down_t)))
    grad_third = scatter_grads(
        left_contract(rows_three, grad_gate_up), left_contract(grad_rows, hidden)
    )
    back_three, gain_three = norm_backward(grad_normed_three, unit_three, inverse_three, gains[2:3])
    grad_stream_two = grad_out.astype(F32) + back_three
    grad_two_rows = spread(to_half(grad_stream_two))
    grad_mixed_cross = to_half(matmul(grad_two_rows, cross_out_t))
    grad_cross = attend_back(cross_qkv, probs_cross, grad_mixed_cross, False)
    grad_q_cross = grad_cross[:, :W]
    grad_kv_cross = grad_cross[:, W:]
    grad_normed_two = collect(right_contract(grad_q_cross, cross_q_w))
    grad_encoder = collect(right_contract(grad_kv_cross, cross_kv_w))
    grad_second = scatter_grads(
        left_contract(rows_two, grad_q_cross),
        left_contract(source_rows, grad_kv_cross),
        left_contract(grad_two_rows, mixed_cross),
    )
    back_two, gain_two = norm_backward(grad_normed_two, unit_two, inverse_two, gains[1:2])
    grad_stream_one = grad_stream_two + back_two
    grad_one_rows = spread(to_half(grad_stream_one))
    grad_mixed_self = to_half(matmul(grad_one_rows, self_out_t))
    grad_self, diagonal = attend_back(self_qkv, probs_self, grad_mixed_self, True)
    grad_normed_one = collect(right_contract(grad_self, self_qkv_w))
    grad_first = scatter_grads(
        left_contract(rows_one, grad_self), left_contract(grad_one_rows, mixed_self)
    )
    back_one, gain_one = norm_backward(grad_normed_one, unit_one, inverse_one, gains[0:1])
    grad_in = grad_stream_one + back_one

    bias_part = jnp.einsum("bm,hm->bh", indicator, diagonal, precision=lax.Precision.HIGHEST)
    tensor_size = lax.axis_size("tensor")
    bias_wide = jnp.where(
        (jnp.arange(tensor_size) == t_index)[:, None], bias_part.reshape(1, -1), 0.0
    )
    small = jnp.concatenate(
        [jnp.stack([gain_one, gain_two, gain_three]).reshape(-1), bias_wide.reshape(-1)]
    )
    small = lax.psum(small, ("dp", "tensor"))
    share = D // (lax.axis_size("dp") * tensor_size)
    place = lax.axis_index("dp") * tensor_size + t_index
    grad_norm_scales = lax.dynamic_slice_in_dim(small[:3 * D].reshape(3, D), place * share, share, 1)
    grad_rel_bias = lax.dynamic_slice_in_dim(
        small[3 * D:].reshape(tensor_size, NBUCKET, heads), t_index, 1, 0
    )[0]
    return (
        layer_out,
        grad_in,
        grad_encoder,
        grad_first[:, :W],
        grad_first[:, W:2 * W],
        grad_first[:, 2 * W:3 * W],
        grad_first[:, 3 * W:].T,
        grad_second[:, :W],
        grad_second[:, W:2 * W],
        grad_second[:, 2 * W:3 * W],
        grad_second[:, 3 * W:].T,
        grad_third[:, :FFL],
        grad_third[:, FFL:2 * FFL],
        grad_third[:, 2 * FFL:].T,
        grad_norm_scales,
        grad_rel_bias,
    )


def solution(mesh):
    in_specs = (
        P(("dp", "tensor"), None),
        P(("dp", "tensor"), None),
        P(("dp", "tensor"), None),
        P("dp", None, None),
        P("dp", None, None),
        P("dp", "tensor"),
        P("dp", "tensor"),
        P("dp", "tensor"),
        P("tensor", "dp"),
        P("dp", "tensor"),
        P("dp", "tensor"),
        P("dp", "tensor"),
        P("tensor", "dp"),
        P("dp", "tensor"),
        P("dp", "tensor"),
        P("tensor", "dp"),
        P(None, "dp"),
        P(None, "tensor"),
    )
    out_specs = (
        P(("dp", "tensor"), None),
        P(("dp", "tensor"), None),
        P(("dp", "tensor"), None),
        P("dp", "tensor"),
        P("dp", "tensor"),
        P("dp", "tensor"),
        P("tensor", "dp"),
        P("dp", "tensor"),
        P("dp", "tensor"),
        P("dp", "tensor"),
        P("tensor", "dp"),
        P("dp", "tensor"),
        P("dp", "tensor"),
        P("tensor", "dp"),
        P(None, ("dp", "tensor")),
        P(None, "tensor"),
    )
    return jax.shard_map(
        per_device, mesh=mesh, in_specs=in_specs, out_specs=out_specs, check_vma=False
    )
```

time: 1380 us -> 582 us (0.42)
  blocking collectives: 471 us -> 102 us
  waiting for transfers between devices: 710 us -> 348 us
  matrix products: 107 us -> 39.3 us
  Pallas kernels: 0 us -> 28 us
  local copies, waits for them, and re-layouts: 41.4 us -> 20.9 us
    reduce_scatter x15 -> x8, waiting for transfers between devices: 676 us -> 155 us  [the longest x7 129 us: collect(): lax.psum_scatter(to_half(partial_rows), 'tensor', scatter_dimension=0, ti...]
    all_gather x12 -> x1, blocking collectives: 307 us -> 25.9 us  [gather_weights(): lax.all_gather(jnp.concatenate(parts, axis=1), 'dp', axis=0, tiled=True)]
    unnamed x20 -> x15, waiting for transfers between devices: 33.1 us -> 122 us
    all_gather x5 -> x4, blocking collectives: 112 us -> 35.2 us  [spread(): return lax.all_gather(rows_local, 'tensor', axis=0, tiled=True)]
    all_gather x0 -> x2, waiting for transfers between devices: none -> 70.8 us  [gather_weights(): lax.all_gather(jnp.concatenate(parts, axis=1), 'dp', axis=0, tiled=True)]
    dot_general x39 -> x9, matrix products: 72.7 us -> 14 us  [the longest x7 13.7 us: matmul(): return jnp.dot(left_side, right_side, preferred_element_type=F32)]
    unnamed x1 -> x0, blocking collectives: 40 us -> none
    psum x1, blocking collectives: 12.5 us -> 40.9 us  [per_device(): small = lax.psum(small, ('dp', 'tensor'))]
  transfers between devices with their start and end apart: 18 -> 13, of which waited for: 15 -> 11; matrix products, arithmetic and copies ran while one was open for 9% -> 9% of each run, Pallas kernels for 0% -> 2%
where the time goes in v1:
time: 582 us; the launch traced here: 577 us
  waiting for transfers between devices  348 us (60%)
  blocking collectives  102 us (18%)
  matrix products  39.3 us (7%)
  Pallas kernels  28 us (5%)
  other arithmetic  23.6 us (4%)
  local copies, waits for them, and re-layouts  20.9 us (4%)
  between operations  14.6 us (3%)
    reduce_scatter x7, waiting for transfers between devices, collect(): lax.psum_scatter(to_half(partial_rows), 'tensor', scatter_dimension=0, ti...  129 us
    unnamed x15, waiting for transfers between devices  122 us
    all_gather x2, waiting for transfers between devices, gather_weights(): lax.all_gather(jnp.concatenate(parts, axis=1), 'dp', axis=0, tiled=True)  70.8 us
    psum x1, blocking collectives, per_device(): small = lax.psum(small, ('dp', 'tensor'))  40.9 us
    all_gather x4, blocking collectives, spread(): return lax.all_gather(rows_local, 'tensor', axis=0, tiled=True)  35.2 us
    reduce_scatter x1, waiting for transfers between devices, scatter_grads(): lax.psum_scatter(to_half(jnp.concatenate(parts, axis=1)), 'dp', scatter_d...  26.5 us
    all_gather x1, blocking collectives, gather_weights(): lax.all_gather(jnp.concatenate(parts, axis=1), 'dp', axis=0, tiled=True)  25.9 us
    dot_general x7, matrix products, right_contract(): lax.dot_general(left_side, right_side, (((1,), (1,)), ((), ())), preferre...  17.5 us
  transfers between devices with their start and end apart: 13, of which 11 were waited for; matrix products, arithmetic and copies ran while one was open for 9% of the time, Pallas kernels for 2%

profile of v1, /device:TPU:13, one launch (start us, length us, event | category | flops | bytes accessed | tf_op | source)
XLA Modules:
  0.0 576.6 jit_solution(3977236910389107628)
XLA Ops:
  12.9 25.9 %all_gather.25 = bf16[768,579]{1,0:T(8,128)(2,1)S(1)} all-gather(bf16[96,579]{1,0:T(8,128)(2,1)S(1)} %pad_maximum_fusion.9), channel_id=1, replica_groups=mesh['dp'=8,'tensor'=4] {'dp'}, dimensions={0}, use_global_device_ids=true | all-gather | bytes 1000512 | tf_op jit(solution)/shard_map/all_gather | solution.py:210
  40.9 2.8 convolution_convert_fusion.10.r_0_
  43.7 6.7 %self_fwd.1 = (bf16[512,192]{1,0:T(8,128)(2,1)}, bf16[3,512,512]{2,1,0:T(8,128)(2,1)}) custom-call(bf16[512,576]{1,0:T(8,128)(2,1)} %convolution_convert_fusion.10.r_0_, f32[3,8,512]{2,1,0:T(8,128)} %stack.47.r_1_, s32[512,512]{1,0:T(8,128)} %bitcast.59), custom_call_target="tpu_custom_call" | custom-call | tf_op jit(solution)/shard_map/self_fwd/pallas_call | solution.py:190
  50.4 29.3 %all-gather.6.cloned.1.call-done = bf16[768,960]{1,0:T(8,128)(2,1)} async-done(((bf16[96,960]{1,0:T(8,128)(2,1)}), bf16[768,960]{1,0:T(8,128)(2,1)}) %all-gather.6.cloned.1.call-update) | async-done | bytes 1474576 | tf_op jit(solution)/shard_map/all_gather | solution.py:210
  84.0 21.9 %reduce-scatter.15.cloned.1.call-done = bf16[128,768]{1,0:T(8,128)(2,1)} async-done(((bf16[512,768]{1,0:T(8,128)(2,1)}), bf16[128,768]{1,0:T(8,128)(2,1)}) %reduce-scatter.15.cloned.1.call-update) | async-done | bytes 196624 | tf_op jit(solution)/shard_map/reduce_scatter | solution.py:65
  108.0 8.7 %all_gather.27 = bf16[512,768]{1,0:T(8,128)(2,1)S(1)} all-gather(bf16[128,768]{1,0:T(8,128)(2,1)S(1)} %multiply_convert_fusion.3), channel_id=1, replica_groups=mesh['dp'=8,'tensor'=4] {'tensor'}, dimensions={0}, use_global_device_ids=true | all-gather | bytes 983040 | tf_op jit(solution)/shard_map/all_gather | solution.py:61
  118.6 6.8 %cross_fwd.1 = (bf16[512,192]{1,0:T(8,128)(2,1)}, bf16[3,512,512]{2,1,0:T(8,128)(2,1)}) custom-call(bf16[512,576]{1,0:T(8,128)(2,1)} %pad_maximum_fusion.6.r_0_), custom_call_target="tpu_custom_call" | custom-call | tf_op jit(solution)/shard_map/cross_fwd/pallas_call | solution.py:189
  128.6 22.4 %reduce-scatter.17.cloned.1.call-done = bf16[128,768]{1,0:T(8,128)(2,1)} async-done(((bf16[512,768]{1,0:T(8,128)(2,1)}), bf16[128,768]{1,0:T(8,128)(2,1)}) %reduce-scatter.17.cloned.1.call-update) | async-done | bytes 196624 | tf_op jit(solution)/shard_map/reduce_scatter | solution.py:65
  153.1 8.9 %all_gather.28 = bf16[512,768]{1,0:T(8,128)(2,1)S(1)} all-gather(bf16[128,768]{1,0:T(8,128)(2,1)S(1)} %multiply_convert_fusion.2), channel_id=1, replica_groups=mesh['dp'=8,'tensor'=4] {'tensor'}, dimensions={0}, use_global_device_ids=true | all-gather | bytes 983040 | tf_op jit(solution)/shard_map/all_gather | solution.py:61
  162.0 41.5 %all-gather.8.cloned.1.call-done = bf16[768,1536]{1,0:T(8,128)(2,1)} async-done(((bf16[96,1536]{1,0:T(8,128)(2,1)}), bf16[768,1536]{1,0:T(8,128)(2,1)}) %all-gather.8.cloned.1.call-update) | async-done | bytes 2359312 | tf_op jit(solution)/shard_map/all_gather | solution.py:210
  206.1 3.2 fusion.12
  212.1 23.7 %reduce-scatter.21.cloned.1.call-done = bf16[128,768]{1,0:T(8,128)(2,1)} async-done(((bf16[512,768]{1,0:T(8,128)(2,1)}), bf16[128,768]{1,0:T(8,128)(2,1)}) %reduce-scatter.21.cloned.1.call-update) | async-done | bytes 196624 | tf_op jit(solution)/shard_map/reduce_scatter | solution.py:65
  238.2 8.7 %all_gather.30 = bf16[512,768]{1,0:T(8,128)(2,1)S(1)} all-gather(bf16[128,768]{1,0:T(8,128)(2,1)S(1)} %fusion.58), channel_id=1, replica_groups=mesh['dp'=8,'tensor'=4] {'tensor'}, dimensions={0}, use_global_device_ids=true | all-gather | bytes 983040 | tf_op jit(solution)/shard_map/all_gather | solution.py:61
  249.2 7.4 %cross_bwd.1 = bf16[512,576]{1,0:T(8,128)(2,1)} custom-call(bf16[512,576]{1,0:T(8,128)(2,1)} %pad_maximum_fusion.6.r_0_, bf16[3,512,512]{2,1,0:T(8,128)(2,1)} %get-tuple-element.24.r_1_, bf16[512,192]{1,0:T(8,128)(2,1)} %copy.128.r_2_), custom_call_target="tpu_custom_call" | custom-call | tf_op jit(solution)/shard_map/cross_bwd/pallas_call | solution.py:204
  259.2 2.9 convolution_convert_fusion.6
  269.1 13.3 %reduce-scatter.23.cloned.1.call-done = bf16[128,768]{1,0:T(8,128)(2,1)} async-done(((bf16[512,768]{1,0:T(8,128)(2,1)}), bf16[128,768]{1,0:T(8,128)(2,1)}) %reduce-scatter.23.cloned.1.call-update) | async-done | bytes 196624 | tf_op jit(solution)/shard_map/reduce_scatter | solution.py:65
  283.6 24.6 %reduce-scatter.19.cloned.1.call-done = bf16[128,768]{1,0:T(8,128)(2,1)} async-done(((bf16[512,768]{1,0:T(8,128)(2,1)}), bf16[128,768]{1,0:T(8,128)(2,1)}) %reduce-scatter.19.cloned.1.call-update) | async-done | bytes 196624 | tf_op jit(solution)/shard_map/reduce_scatter | solution.py:65
  310.2 8.9 %all_gather.31 = bf16[512,768]{1,0:T(8,128)(2,1)S(1)} all-gather(bf16[128,768]{1,0:T(8,128)(2,1)S(1)} %get-tuple-element.102), channel_id=1, replica_groups=mesh['dp'=8,'tensor'=4] {'tensor'}, dimensions={0}, use_global_device_ids=true | all-gather | bytes 983040 | tf_op jit(solution)/shard_map/all_gather | solution.py:61
  321.4 7.1 %self_bwd.1 = (bf16[512,576]{1,0:T(8,128)(2,1)}, f32[3,512]{1,0:T(4,128)}) custom-call(bf16[512,576]{1,0:T(8,128)(2,1)} %convolution_convert_fusion.10.r_0_, bf16[3,512,512]{2,1,0:T(8,128)(2,1)} %get-tuple-element.25.r_1_, bf16[512,192]{1,0:T(8,128)(2,1)} %copy.129.r_2_), custom_call_target="tpu_custom_call" | custom-call | tf_op jit(solution)/shard_map/self_bwd/pallas_call | solution.py:198
  343.0 57.0 %reduce-scatter.33.cloned.1.call-done = bf16[96,768]{1,0:T(8,128)(2,1)} async-done(((bf16[768,768]{1,0:T(8,128)(2,1)}), bf16[96,768]{1,0:T(8,128)(2,1)}) %reduce-scatter.33.cloned.1.call-update) | async-done | bytes 147472
  404.0 22.8 %reduce-scatter.25.cloned.1.call-done = bf16[128,768]{1,0:T(8,128)(2,1)} async-done(((bf16[512,768]{1,0:T(8,128)(2,1)}), bf16[128,768]{1,0:T(8,128)(2,1)}) %reduce-scatter.25.cloned.1.call-update) | async-done | bytes 196624 | tf_op jit(solution)/shard_map/reduce_scatter | solution.py:65
  428.1 40.9 %psum.7 = f32[2688]{0:T(1024)S(1)} all-reduce(f32[2688]{0:T(1024)S(1)} %pad_maximum_fusion.11), channel_id=1, replica_groups=mesh['dp'=8,'tensor'=4] {'dp','tensor'}, use_global_device_ids=true, to_apply=%region_20.21 | all-reduce | flops 2688 | bytes 21504 | tf_op jit(solution)/shard_map/psum | solution.py:326
  472.5 26.5 %reduce-scatter.29.cloned.1.call-done = bf16[96,1536]{1,0:T(8,128)(2,1)} async-done(((bf16[768,1536]{1,0:T(8,128)(2,1)}), bf16[96,1536]{1,0:T(8,128)(2,1)}) %reduce-scatter.29.cloned.1.call-update) | async-done | bytes 294928 | tf_op jit(solution)/shard_map/reduce_scatter | solution.py:214
  501.8 64.3 %reduce-scatter.31.cloned.1.call-done = bf16[96,768]{1,0:T(8,128)(2,1)} async-done(((bf16[768,768]{1,0:T(8,128)(2,1)}), bf16[96,768]{1,0:T(8,128)(2,1)}) %reduce-scatter.31.cloned.1.call-update) | async-done | bytes 147472
  (208 shorter events, 75.7 us)
Async XLA Ops:
  7.3 5.5 copy-start.21
  7.3 32.2 %all-gather.4.cloned.1.call-start = ((), (), s32[]{:S(2)}) async-start(), calls=%async_computation.10 | async-start | bytes 2949120 | tf_op jit(solution)/shard_map/all_gather | solution.py:61
  9.4 70.2 %all-gather.6.cloned.1.call-start = ((), (), s32[]{:S(2)}) async-start(), calls=%async_computation.11 | async-start | bytes 1769472 | tf_op jit(solution)/shard_map/all_gather | solution.py:210
  10.6 95.3 %reduce-scatter.15.cloned.1.call-start = ((), (), s32[]{:S(2)}) async-start(), calls=%async_computation.12 | async-start | bytes 983040 | tf_op jit(solution)/shard_map/reduce_scatter | solution.py:65
  82.2 23.8 %copy-start.1 = (bf16[128,768]{1,0:T(8,128)(2,1)S(1)}, bf16[128,768]{1,0:T(8,128)(2,1)}, u32[]{:S(2)}) copy-start(bf16[128,768]{1,0:T(8,128)(2,1)} %param.19) | copy-start | bytes 589828
  82.2 68.8 %reduce-scatter.17.cloned.1.call-start = ((), (), s32[]{:S(2)}) async-start(), calls=%async_computation.13 | async-start | bytes 983040 | tf_op jit(solution)/shard_map/reduce_scatter | solution.py:65
  118.6 9.2 %copy-start.15 = (bf16[512,96]{0,1:T(8,128)(2,1)S(1)}, bf16[512,96]{0,1:T(8,128)(2,1)}, u32[]{:S(2)}) copy-start(bf16[512,96]{0,1:T(8,128)(2,1)} %param.33) | copy-start | bytes 294916
  118.6 9.2 %copy-start.16 = (bf16[96,512]{1,0:T(8,128)(2,1)S(1)}, bf16[96,512]{1,0:T(8,128)(2,1)}, u32[]{:S(2)}) copy-start(bf16[96,512]{1,0:T(8,128)(2,1)} %param.32) | copy-start | bytes 294916
  118.6 9.2 %copy-start.17 = (bf16[96,512]{1,0:T(8,128)(2,1)S(1)}, bf16[96,512]{1,0:T(8,128)(2,1)}, u32[]{:S(2)}) copy-start(bf16[96,512]{1,0:T(8,128)(2,1)} %param.31) | copy-start | bytes 294916
  125.4 25.6 %copy-start.2 = (bf16[128,768]{1,0:T(8,128)(2,1)S(1)}, bf16[128,768]{1,0:T(8,128)(2,1)}, u32[]{:S(2)}) copy-start(bf16[128,768]{1,0:T(8,128)(2,1)} %reduce-scatter.15.cloned.1.call-done) | copy-start | bytes 589828
  127.7 75.8 %all-gather.8.cloned.1.call-start = ((), (), s32[]{:S(2)}) async-start(), calls=%async_computation.14 | async-start | bytes 2654208 | tf_op jit(solution)/shard_map/all_gather | solution.py:210
  128.6 107.3 %reduce-scatter.21.cloned.1.call-start = ((), (), s32[]{:S(2)}) async-start(), calls=%async_computation.16 | async-start | bytes 983040 | tf_op jit(solution)/shard_map/reduce_scatter | solution.py:65
  162.0 44.1 %copy-start.12 = (bf16[512,768]{1,0:T(8,128)(2,1)}, bf16[512,768]{1,0:T(8,128)(2,1)S(1)}, u32[]{:S(2)}) copy-start(bf16[512,768]{1,0:T(8,128)(2,1)S(1)} %all_gather.28) | copy-start | bytes 2359300
  210.1 25.7 %copy-start.3 = (bf16[128,768]{1,0:T(8,128)(2,1)S(1)}, bf16[128,768]{1,0:T(8,128)(2,1)}, u32[]{:S(2)}) copy-start(bf16[128,768]{1,0:T(8,128)(2,1)} %reduce-scatter.17.cloned.1.call-done) | copy-start | bytes 589828
  212.1 25.0 %copy-start.6 = (bf16[128,768]{1,0:T(8,128)(2,1)S(1)}, bf16[128,768]{1,0:T(8,128)(2,1)}, u32[]{:S(2)}) copy-start(bf16[128,768]{1,0:T(8,128)(2,1)} %param.21) | copy-start | bytes 589828
  212.1 70.3 %reduce-scatter.23.cloned.1.call-start = ((), (), s32[]{:S(2)}) async-start(), calls=%async_computation.17 | async-start | bytes 983040 | tf_op jit(solution)/shard_map/reduce_scatter | solution.py:65
  259.1 49.0 %reduce-scatter.19.cloned.1.call-start = ((), (), s32[]{:S(2)}) async-start(), calls=%async_computation.15 | async-start | bytes 983040 | tf_op jit(solution)/shard_map/reduce_scatter | solution.py:65
  262.1 79.2 %reduce-scatter.27.cloned.1.call-start = ((), (), s32[]{:S(2)}) async-start(), calls=%async_computation.19 | async-start | bytes 983040 | tf_op jit(solution)/shard_map/reduce_scatter | solution.py:65
  264.8 135.3 %reduce-scatter.33.cloned.1.call-start = ((), (), s32[]{:S(2)}) async-start(), calls=%async_computation.22 | async-start | bytes 1327104
  267.5 40.7 %copy-start.7 = (bf16[128,768]{1,0:T(8,128)(2,1)S(1)}, bf16[128,768]{1,0:T(8,128)(2,1)}, u32[]{:S(2)}) copy-start(bf16[128,768]{1,0:T(8,128)(2,1)} %reduce-scatter.21.cloned.1.call-done) | copy-start | bytes 589828
  269.0 157.9 %reduce-scatter.25.cloned.1.call-start = ((), (), s32[]{:S(2)}) async-start(), calls=%async_computation.18 | async-start | bytes 983040 | tf_op jit(solution)/shard_map/reduce_scatter | solution.py:65
  320.6 7.9 %copy-start.9 = (bf16[768,579]{1,0:T(8,128)(2,1)S(1)}, bf16[768,579]{1,0:T(8,128)(2,1)}, u32[]{:S(2)}) copy-start(bf16[768,579]{1,0:T(8,128)(2,1)} %copy-done.8) | copy-start | bytes 2668036
  331.3 167.7 %reduce-scatter.29.cloned.1.call-start = ((), (), s32[]{:S(2)}) async-start(), calls=%async_computation.20 | async-start | bytes 2654208 | tf_op jit(solution)/shard_map/reduce_scatter | solution.py:214
  336.1 230.0 %reduce-scatter.31.cloned.1.call-start = ((), (), s32[]{:S(2)}) async-start(), calls=%async_computation.21 | async-start | bytes 1327104
  (23 other events, 63.4 us)
Sparse Core Ops, SparseCore 0:
  9.7 25.5 all-gather.3
  38.0 41.6 all-gather.5
  82.3 23.5 reduce-scatter.14
  127.9 23.0 reduce-scatter.16
  153.6 49.9 all-gather.7
  212.2 23.5 reduce-scatter.20
  259.3 23.0 reduce-scatter.22
  284.9 23.2 reduce-scatter.18
  310.7 23.1 reduce-scatter.26
  337.2 62.8 reduce-scatter.32
  402.6 24.2 reduce-scatter.24
  430.2 68.7 reduce-scatter.28
  502.4 63.6 reduce-scatter.30

commit v2 on v1

--- a/solution.py
+++ b/solution.py
@@ -179,6 +179,241 @@
             diag_ref[h:h + 1, :] = total
 
 
+MESH = pl.DeviceIdType.MESH
+
+
+def tensor_place():
+    me = lax.axis_index("tensor")
+    partner = me + 1 - 2 * lax.rem(me, 2)
+    across = lax.rem(me + 2, 4)
+    return me, partner, across
+
+
+def greet(*peers):
+    barrier = pltpu.get_barrier_semaphore()
+    for peer in peers:
+        pl.semaphore_signal(barrier, inc=1, device_id=peer, device_id_type=MESH)
+    pl.semaphore_wait(barrier, len(peers))
+
+
+def remote(source, target, sems, index, peer):
+    copy = pltpu.make_async_remote_copy(
+        src_ref=source,
+        dst_ref=target,
+        send_sem=sems[0].at[index],
+        recv_sem=sems[1].at[index],
+        device_id={"tensor": peer},
+        device_id_type=MESH,
+    )
+    copy.start()
+    return copy
+
+
+def reduce_rows(lhs_ref, w_ref, sent, landed, sems):
+    me, partner, across = tensor_place()
+    share = landed.shape[1]
+
+    def part(block):
+        return right_contract(lhs_ref[pl.ds(pl.multiple_of(block * share, share), share), :], w_ref[...])
+
+    sent[0] = to_half(part(lax.rem(partner + 2, 4)))
+    far = remote(sent.at[0], landed.at[0], sems, 0, partner)
+    sent[1] = to_half(part(partner))
+    near = remote(sent.at[1], landed.at[1], sems, 1, partner)
+    mine_far = part(across)
+    far.wait()
+    sent[2] = to_half(mine_far + landed[0].astype(F32))
+    over = remote(sent.at[2], landed.at[2], sems, 2, across)
+    mine = part(me)
+    near.wait()
+    mine = mine + landed[1].astype(F32)
+    over.wait()
+    return mine + landed[2].astype(F32)
+
+
+def spread_rows(rows, held, rows_ref, sems):
+    me, partner, across = tensor_place()
+    share = rows.shape[0]
+
+    def block(index):
+        return held.at[pl.ds(pl.multiple_of(index * share, share), share)]
+
+    held[pl.ds(pl.multiple_of(me * share, share), share), :] = rows
+    over = remote(block(me), block(me), sems, 3, across)
+    near = remote(block(me), block(me), sems, 4, partner)
+    over.wait()
+    forward = remote(block(across), block(across), sems, 5, partner)
+    near.wait()
+    forward.wait()
+    rows_ref[...] = held[...]
+
+
+def forward_kernel(lhs_ref, w_ref, stream_ref, gain_ref, rows_ref, out_ref, sent, landed, held, send, recv):
+    me, partner, across = tensor_place()
+    greet({"tensor": partner}, {"tensor": across})
+    stream = stream_ref[...].astype(F32) + reduce_rows(lhs_ref, w_ref, sent, landed, (send, recv))
+    out_ref[...] = stream
+    spread_rows(to_half(unit_norm(stream)[0] * gain_ref[...]), held, rows_ref, (send, recv))
+
+
+def backward_kernel(spreading, lhs_ref, w_ref, stream_ref, grad_ref, gain_ref, *refs):
+    if spreading:
+        rows_ref, out_ref, gain_out, sent, landed, held, send, recv = refs
+    else:
+        out_ref, gain_out, sent, landed, send, recv = refs
+    me, partner, across = tensor_place()
+    greet({"tensor": partner}, {"tensor": across})
+    unit, inverse = unit_norm(stream_ref[...].astype(F32))
+    incoming = reduce_rows(lhs_ref, w_ref, sent, landed, (send, recv))
+    back, gain_grad = norm_backward(incoming, unit, inverse, gain_ref[...])
+    grad = grad_ref[...].astype(F32) + back
+    out_ref[...] = grad
+    gain_out[...] = gain_grad[None]
+    if spreading:
+        spread_rows(to_half(grad), held, rows_ref, (send, recv))
+
+
+def exchange(kernel, number, outs, share, width, rows, *operands):
+    count = 6 if rows else 3
+    scratch = [pltpu.VMEM((3, share, width), BF16), pltpu.VMEM((3, share, width), BF16)]
+    if rows:
+        scratch.append(pltpu.VMEM((rows, width), BF16))
+    scratch += [pltpu.SemaphoreType.DMA((count,)), pltpu.SemaphoreType.DMA((count,))]
+    return pl.pallas_call(
+        kernel,
+        out_shape=outs,
+        scratch_shapes=scratch,
+        name=f"exchange_{number}",
+        compiler_params=pltpu.CompilerParams(
+            collective_id=number, has_side_effects=True, vmem_limit_bytes=60 * 1024 * 1024
+        ),
+    )(*operands)
+
+
+def forward_exchange(number, lhs, w, stream, gain):
+    share, width = stream.shape
+    outs = (whole((L, width), BF16), whole((share, width), F32))
+    return exchange(forward_kernel, number, outs, share, width, L, lhs, w, stream, gain)
+
+
+def backward_exchange(number, spreading, lhs, w, stream, grad, gain):
+    share, width = stream.shape
+    outs = (whole((share, width), F32), whole((1, width), F32))
+    if spreading:
+        outs = (whole((L, width), BF16),) + outs
+
+    def kernel(*refs):
+        backward_kernel(spreading, *refs)
+
+    return exchange(
+        kernel, number, outs, share, width, L if spreading else 0, lhs, w, stream, grad, gain
+    )
+
+
+def sum_kernel(grads_ref, small_ref, out_ref, small_out, landed, small_landed, small_sum, gain_landed, *sems):
+    send, recv, small_send, small_recv, gain_send, gain_recv = sems
+    n = grads_ref.shape[0]
+    me = lax.axis_index("dp")
+    column = lax.axis_index("tensor")
+    barrier = pltpu.get_barrier_semaphore()
+
+    def hello(o, carry):
+        pl.semaphore_signal(barrier, inc=1, device_id={"dp": lax.rem(me + o, n)}, device_id_type=MESH)
+        return carry
+
+    lax.fori_loop(1, n, hello, 0)
+    for o in range(1, 4):
+        pl.semaphore_signal(barrier, inc=1, device_id={"tensor": lax.rem(column + o, 4)}, device_id_type=MESH)
+    pl.semaphore_wait(barrier, n - 1 + 3)
+
+    def copies(o):
+        peer = lax.rem(me + o, n)
+        big = pltpu.make_async_remote_copy(
+            src_ref=grads_ref.at[peer],
+            dst_ref=landed.at[o],
+            send_sem=send.at[o],
+            recv_sem=recv.at[o],
+            device_id={"dp": peer},
+            device_id_type=MESH,
+        )
+        little = pltpu.make_async_remote_copy(
+            src_ref=small_ref.at[peer],
+            dst_ref=small_landed.at[o],
+            send_sem=small_send.at[o],
+            recv_sem=small_recv.at[o],
+            device_id={"dp": peer},
+            device_id_type=MESH,
+        )
+        return big, little
+
+    def launch_small(o, carry):
+        copies(o)[1].start()
+        return carry
+
+    def launch(o, carry):
+        copies(o)[0].start()
+        return carry
+
+    def finish_small(o, total):
+        copies(o)[1].wait()
+        return total + small_landed[o]
+
+    lax.fori_loop(1, n, launch_small, 0)
+    lax.fori_loop(1, n, launch, 0)
+    small = lax.fori_loop(1, n, finish_small, small_ref[me])
+    small_sum[...] = small
+    gain_copies = []
+    for o in range(1, 4):
+        copy = pltpu.make_async_remote_copy(
+            src_ref=small_sum,
+            dst_ref=gain_landed.at[o],
+            send_sem=gain_send.at[o],
+            recv_sem=gain_recv.at[o],
+            device_id={"tensor": lax.rem(column + o, 4)},
+            device_id_type=MESH,
+        )
+        copy.start()
+        gain_copies.append(copy)
+    small_out[0] = small
+    for o, copy in enumerate(gain_copies, 1):
+        copy.wait()
+        small = small + gain_landed[o]
+    small_out[1] = small
+    out_ref[...] = grads_ref[me].astype(F32)
+
+    def finish(o, carry):
+        copies(o)[0].wait()
+        out_ref[...] += landed[o].astype(F32)
+        return carry
+
+    lax.fori_loop(1, n, finish, 0)
+
+
+def sum_over_dp(number, grads, small):
+    n, rows, width = grads.shape
+    dma = pltpu.SemaphoreType.DMA
+    return pl.pallas_call(
+        sum_kernel,
+        out_shape=(whole((rows, width), F32), whole((2,) + small.shape[1:], F32)),
+        scratch_shapes=[
+            pltpu.VMEM(grads.shape, BF16),
+            pltpu.VMEM(small.shape, F32),
+            pltpu.VMEM(small.shape[1:], F32),
+            pltpu.VMEM((4,) + small.shape[1:], F32),
+            dma((n,)),
+            dma((n,)),
+            dma((n,)),
+            dma((n,)),
+            dma((4,)),
+            dma((4,)),
+        ],
+        name="sum_over_dp",
+        compiler_params=pltpu.CompilerParams(
+            collective_id=number, has_side_effects=True, vmem_limit_bytes=60 * 1024 * 1024
+        ),
+    )(grads, small)
+
+
 def attend(qkv, base, keep):
     width = qkv.shape[1] // 3
     outs = (
@@ -237,45 +472,38 @@
     W = wq_self.shape[1]
     FFL = w_gate.shape[1]
     D = layer_in.shape[1]
-    RL = layer_in.shape[0]
     heads = W // DH
     t_index = lax.axis_index("tensor")
     indicator = jnp.asarray(distance_indicator())
     base_row = jnp.einsum("bm,bh->hm", indicator, rel_bias, precision=lax.Precision.HIGHEST)
     base = jnp.stack([jnp.roll(base_row, s, axis=1) for s in range(8)], axis=1)
 
-    first = gather_weights(wq_self, wk_self, wv_self, norm_scales.T)
-    rows_all = spread(jnp.concatenate([layer_in, encoder_states, grad_out], axis=1))
-    second = gather_weights(wo_self.T, wq_cross, wk_cross, wv_cross, wo_cross.T)
-    third = gather_weights(w_gate, w_up, w_down.T)
+    first = gather_weights(
+        wq_self, wk_self, wv_self, wo_self.T, wq_cross, wk_cross, wv_cross, wo_cross.T, norm_scales.T
+    )
+    stream_all = spread(layer_in)
+    others = spread(jnp.concatenate([encoder_states, grad_out], axis=1))
+    second = gather_weights(w_gate, w_up, w_down.T)
     self_qkv_w = first[:, :3 * W]
-    gains = first[:, 3 * W:].T.astype(F32)
-    self_out_t = second[:, :W]
-    cross_q_w = second[:, W:2 * W]
-    cross_kv_w = second[:, 2 * W:4 * W]
-    cross_out_t = second[:, 4 * W:]
-    gate_up_w = third[:, :2 * FFL]
-    down_t = third[:, 2 * FFL:]
-
-    stream_all = rows_all[:, :D]
-    source_rows = rows_all[:, D:2 * D]
-    grad_rows = rows_all[:, 2 * D:]
+    self_out_t = first[:, 3 * W:4 * W]
+    cross_q_w = first[:, 4 * W:5 * W]
+    cross_kv_w = first[:, 5 * W:7 * W]
+    cross_out_t = first[:, 7 * W:8 * W]
+    gains = first[:, 8 * W:].T.astype(F32)
+    gate_up_w = second[:, :2 * FFL]
+    down_t = second[:, 2 * FFL:]
+    source_rows = others[:, :D]
+    grad_rows = others[:, D:]
+
     rows_one = to_half(unit_norm(stream_all.astype(F32))[0] * gains[0:1])
-    stream_in = layer_in.astype(F32)
-    unit_one, inverse_one = unit_norm(stream_in)
-
     self_qkv = to_half(matmul(rows_one, self_qkv_w))
     mixed_self, probs_self = attend(self_qkv, base, keep[0])
-    stream_one = stream_in + collect(right_contract(mixed_self, self_out_t))
-    unit_two, inverse_two = unit_norm(stream_one)
-    rows_two = spread(to_half(unit_two * gains[1:2]))
+    rows_two, stream_one = forward_exchange(1, mixed_self, self_out_t, layer_in, gains[1:2])
     cross_qkv = jnp.concatenate(
         [to_half(matmul(rows_two, cross_q_w)), to_half(matmul(source_rows, cross_kv_w))], axis=1
     )
     mixed_cross, probs_cross = attend(cross_qkv, None, None)
-    stream_two = stream_one + collect(right_contract(mixed_cross, cross_out_t))
-    unit_three, inverse_three = unit_norm(stream_two)
-    rows_three = spread(to_half(unit_three * gains[2:3]))
+    rows_three, stream_two = forward_exchange(2, mixed_cross, cross_out_t, stream_one, gains[2:3])
     gate_up = matmul(rows_three, gate_up_w)
     up_rows = gate_up[:, FFL:]
     activated, slope = gelu_pair(gate_up[:, :FFL])
@@ -284,52 +512,61 @@
     grad_gate_up = to_half(
         jnp.concatenate([grad_hidden * up_rows * slope, grad_hidden * activated], axis=1)
     )
-    grad_normed_three = collect(right_contract(grad_gate_up, gate_up_w))
-    layer_out = to_half(stream_two + collect(right_contract(hidden, down_t)))
+    grad_two_rows, grad_stream_two, gain_three = backward_exchange(
+        3, True, grad_gate_up, gate_up_w, stream_two, grad_out, gains[2:3]
+    )
     grad_third = scatter_grads(
         left_contract(rows_three, grad_gate_up), left_contract(grad_rows, hidden)
     )
-    back_three, gain_three = norm_backward(grad_normed_three, unit_three, inverse_three, gains[2:3])
-    grad_stream_two = grad_out.astype(F32) + back_three
-    grad_two_rows = spread(to_half(grad_stream_two))
+    layer_out = to_half(stream_two + collect(right_contract(hidden, down_t)))
     grad_mixed_cross = to_half(matmul(grad_two_rows, cross_out_t))
     grad_cross = attend_back(cross_qkv, probs_cross, grad_mixed_cross, False)
     grad_q_cross = grad_cross[:, :W]
     grad_kv_cross = grad_cross[:, W:]
-    grad_normed_two = collect(right_contract(grad_q_cross, cross_q_w))
+    grad_one_rows, grad_stream_one, gain_two = backward_exchange(
+        4, True, grad_q_cross, cross_q_w, stream_one, grad_stream_two, gains[1:2]
+    )
     grad_encoder = collect(right_contract(grad_kv_cross, cross_kv_w))
-    grad_second = scatter_grads(
-        left_contract(rows_two, grad_q_cross),
-        left_contract(source_rows, grad_kv_cross),
-        left_contract(grad_two_rows, mixed_cross),
-    )
-    back_two, gain_two = norm_backward(grad_normed_two, unit_two, inverse_two, gains[1:2])
-    grad_stream_one = grad_stream_two + back_two
-    grad_one_rows = spread(to_half(grad_stream_one))
     grad_mixed_self = to_half(matmul(grad_one_rows, self_out_t))
     grad_self, diagonal = attend_back(self_qkv, probs_self, grad_mixed_self, True)
-    grad_normed_one = collect(right_contract(grad_self, self_qkv_w))
-    grad_first = scatter_grads(
-        left_contract(rows_one, grad_self), left_contract(grad_one_rows, mixed_self)
-    )
-    back_one, gain_one = norm_backward(grad_normed_one, unit_one, inverse_one, gains[0:1])
-    grad_in = grad_stream_one + back_one
-
+    grad_in, gain_one = backward_exchange(
+        5, False, grad_self, self_qkv_w, layer_in, grad_stream_one, gains[0:1]
+    )
     bias_part = jnp.einsum("bm,hm->bh", indicator, diagonal, precision=lax.Precision.HIGHEST)
+    dp_size = lax.axis_size("dp")
     tensor_size = lax.axis_size("tensor")
-    bias_wide = jnp.where(
-        (jnp.arange(tensor_size) == t_index)[:, None], bias_part.reshape(1, -1), 0.0
-    )
+    share = D // dp_size
+    grads = jnp.concatenate(
+        [
+            to_half(part)
+            for part in (
+                left_contract(rows_one, grad_self),
+                left_contract(grad_one_rows, mixed_self),
+                left_contract(rows_two, grad_q_cross),
+                left_contract(source_rows, grad_kv_cross),
+                left_contract(grad_two_rows, mixed_cross),
+            )
+        ],
+        axis=1,
+    ).reshape(dp_size, share, 8 * W)
+    gain_part = jnp.concatenate([gain_one, gain_two, gain_three]).reshape(3, dp_size, share)
     small = jnp.concatenate(
-        [jnp.stack([gain_one, gain_two, gain_three]).reshape(-1), bias_wide.reshape(-1)]
-    )
-    small = lax.psum(small, ("dp", "tensor"))
-    share = D // (lax.axis_size("dp") * tensor_size)
-    place = lax.axis_index("dp") * tensor_size + t_index
-    grad_norm_scales = lax.dynamic_slice_in_dim(small[:3 * D].reshape(3, D), place * share, share, 1)
-    grad_rel_bias = lax.dynamic_slice_in_dim(
-        small[3 * D:].reshape(tensor_size, NBUCKET, heads), t_index, 1, 0
-    )[0]
+        [
+            jnp.pad(gain_part.transpose(1, 0, 2), ((0, 0), (0, 0), (0, 128 - share))),
+            jnp.broadcast_to(
+                jnp.pad(bias_part.reshape(1, 1, -1), ((0, 0), (0, 0), (0, 128 - NBUCKET * heads))),
+                (dp_size, 1, 128),
+            ),
+            jnp.zeros((dp_size, 4, 128), F32),
+        ],
+        axis=1,
+    )
+    summed, small_sums = sum_over_dp(6, grads, small)
+    grad_first = summed[:, :4 * W]
+    grad_second = summed[:, 4 * W:]
+    own = share // tensor_size
+    grad_norm_scales = lax.dynamic_slice_in_dim(small_sums[1, :3], t_index * own, own, 1)
+    grad_rel_bias = small_sums[0, 3, :NBUCKET * heads].reshape(NBUCKET, heads)
     return (
         layer_out,
         grad_in,

time: 582 us -> 410 us (0.70)
  waiting for transfers between devices: 348 us -> 109 us
  Pallas kernels: 28 us -> 201 us
  blocking collectives: 102 us -> 9.1 us
  matrix products: 39.3 us -> 28.4 us
  other arithmetic: 23.6 us -> 13.2 us
  local copies, waits for them, and re-layouts: 20.9 us -> 29 us
    pallas_call x0 -> x6, Pallas kernels: none -> 173 us  [the longest x5 96.2 us: exchange(): pl.pallas_call(kernel, out_shape=outs, scratch_shapes=scratch, name=f'exc...]
    reduce_scatter x7 -> x2, waiting for transfers between devices: 129 us -> 0.01 us  [collect(): lax.psum_scatter(to_half(partial_rows), 'tensor', scatter_dimension=0, ti...]
    unnamed x15 -> x6, waiting for transfers between devices: 122 us -> 0.1 us
    psum x1 -> x0, blocking collectives: 40.9 us -> none  [per_device(): small = lax.psum(small, ('dp', 'tensor'))]
    all_gather x4 -> x1, blocking collectives: 35.2 us -> 9.1 us  [spread(): return lax.all_gather(rows_local, 'tensor', axis=0, tiled=True)]
    all_gather x1 -> x0, blocking collectives: 25.9 us -> none  [gather_weights(): lax.all_gather(jnp.concatenate(parts, axis=1), 'dp', axis=0, tiled=True)]
    all_gather x2, waiting for transfers between devices: 70.8 us -> 87.5 us  [gather_weights(): lax.all_gather(jnp.concatenate(parts, axis=1), 'dp', axis=0, tiled=True)]
    dot_general x7 -> x2, matrix products: 17.5 us -> 5.48 us  [right_contract(): lax.dot_general(left_side, right_side, (((1,), (1,)), ((), ())), preferre...]
  transfers between devices with their start and end apart: 13 -> 6, of which waited for: 11 -> 3; matrix products, arithmetic and copies ran while one was open for 9% -> 12% of each run, Pallas kernels for 2% -> 36%
where the time goes in v2:
time: 410 us; the launch traced here: 405 us
  Pallas kernels  201 us (49%)
  waiting for transfers between devices  109 us (27%)
  local copies, waits for them, and re-layouts  29 us (7%)
  matrix products  28.4 us (7%)
  between operations  14.7 us (4%)
  other arithmetic  13.2 us (3%)
  blocking collectives  9.1 us (2%)
    pallas_call x5, Pallas kernels, exchange(): pl.pallas_call(kernel, out_shape=outs, scratch_shapes=scratch, name=f'exc...  96.2 us
    all_gather x2, waiting for transfers between devices, gather_weights(): lax.all_gather(jnp.concatenate(parts, axis=1), 'dp', axis=0, tiled=True)  87.5 us
    pallas_call x1, Pallas kernels, sum_over_dp(): pl.pallas_call(sum_kernel, out_shape=(whole((rows, width), F32), whole((2...  76.5 us
    reduce_scatter x1, waiting for transfers between devices, scatter_grads(): lax.psum_scatter(to_half(jnp.concatenate(parts, axis=1)), 'dp', scatter_d...  21.9 us
    dot_general x7, matrix products, matmul(): return jnp.dot(left_side, right_side, preferred_element_type=F32)  15.7 us
    all_gather x1, blocking collectives, spread(): return lax.all_gather(rows_local, 'tensor', axis=0, tiled=True)  9.1 us
  transfers between devices with their start and end apart: 6, of which 3 were waited for; matrix products, arithmetic and copies ran while one was open for 12% of the time, Pallas kernels for 36%

profile of v2, /device:TPU:13, one launch (start us, length us, event | category | flops | bytes accessed | tf_op | source)
XLA Modules:
  0.0 404.9 jit_solution(3706330896224992328)
XLA Ops:
  16.6 9.1 %all_gather.12 = bf16[512,768]{1,0:T(8,128)(2,1)S(1)} all-gather(bf16[128,768]{1,0:T(8,128)(2,1)S(1)} %copy-done.4), channel_id=1, replica_groups=mesh['dp'=8,'tensor'=4] {'tensor'}, dimensions={0}, use_global_device_ids=true | all-gather | bytes 983040 | tf_op jit(solution)/shard_map/all_gather | solution.py:61
  25.9 35.3 %all-gather.8.cloned.1.call-done = bf16[768,1536]{1,0:T(8,128)(2,1)} async-done(((bf16[96,1536]{1,0:T(8,128)(2,1)}), bf16[768,1536]{1,0:T(8,128)(2,1)}) %all-gather.8.cloned.1.call-update) | async-done | bytes 2359312 | tf_op jit(solution)/shard_map/all_gather | solution.py:445
  61.2 2.7 slice.227.refs_1_
  63.9 52.3 %all-gather.4.cloned.1.call-done = bf16[768,1539]{1,0:T(8,128)(2,1)} async-done(((bf16[96,1539]{1,0:T(8,128)(2,1)}), bf16[768,1539]{1,0:T(8,128)(2,1)}) %all-gather.4.cloned.1.call-update) | async-done | bytes 2363920 | tf_op jit(solution)/shard_map/all_gather | solution.py:445
  117.9 3.1 convolution_convert_fusion.5.r_0_
  121.0 6.8 %self_fwd.1 = (bf16[512,192]{1,0:T(8,128)(2,1)}, bf16[3,512,512]{2,1,0:T(8,128)(2,1)}) custom-call(bf16[512,576]{1,0:T(8,128)(2,1)} %convolution_convert_fusion.5.r_0_, f32[3,8,512]{2,1,0:T(8,128)} %stack.35.r_1_, s32[512,512]{1,0:T(8,128)} %bitcast.60), custom_call_target="tpu_custom_call" | custom-call | tf_op jit(solution)/shard_map/self_fwd/pallas_call | solution.py:425
  129.1 20.6 %exchange_1.1 = (bf16[512,768]{1,0:T(8,128)(2,1)}, f32[128,768]{1,0:T(8,128)}) custom-call(bf16[512,192]{1,0:T(8,128)(2,1)} %get-tuple-element.36.lhs_ref, bf16[768,192]{1,0:T(8,128)(2,1)} %get-tuple-element.124.w_ref, bf16[128,768]{1,0:T(8,128)(2,1)} %refs_2_.1, f32[1,768]{1,0:T(1,128)} %get-tuple-element.139.gain_ref.refs_4_), custom_call_target="tpu_custom_call" | custom-call | tf_op jit(solution)/shard_map/exchange_1/pallas_call | solution.py:282
  155.0 6.7 %cross_fwd.1 = (bf16[512,192]{1,0:T(8,128)(2,1)}, bf16[3,512,512]{2,1,0:T(8,128)(2,1)}) custom-call(bf16[512,576]{1,0:T(8,128)(2,1)} %pad_maximum_fusion.2.r_0_), custom_call_target="tpu_custom_call" | custom-call | tf_op jit(solution)/shard_map/cross_fwd/pallas_call | solution.py:424
  161.8 19.2 %exchange_2.1 = (bf16[512,768]{1,0:T(8,128)(2,1)}, f32[128,768]{1,0:T(8,128)}) custom-call(bf16[512,192]{1,0:T(8,128)(2,1)} %get-tuple-element.38.lhs_ref, bf16[768,192]{1,0:T(8,128)(2,1)} %get-tuple-element.123.w_ref, f32[128,768]{1,0:T(8,128)} %get-tuple-element.39.stream_ref.refs_2_, f32[1,768]{1,0:T(1,128)} %get-tuple-element.138.gain_ref.refs_4_), custom_call_target="tpu_custom_call" | custom-call | tf_op jit(solution)/shard_map/exchange_2/pallas_call | solution.py:282
  181.0 2.7 fusion.34
  183.7 3.1 fusion.14
  188.8 19.7 %exchange_3.1 = (bf16[512,768]{1,0:T(8,128)(2,1)}, f32[128,768]{1,0:T(8,128)}, f32[1,768]{1,0:T(1,128)}) custom-call(bf16[512,1024]{1,0:T(8,128)(2,1)} %pad_maximum_fusion.1.refs_0_, bf16[768,1024]{1,0:T(8,128)(2,1)} %slice.227.refs_1_, f32[128,768]{1,0:T(8,128)} %get-tuple-element.40.refs_2_, bf16[128,768]{1,0:T(8,128)(2,1)} %refs_3_.1, ...), custom_call_target="tpu_custom_call" | custom-call | tf_op jit(solution)/shard_map/exchange_3/pallas_call | solution.py:282
  211.0 7.4 %cross_bwd.1 = bf16[512,576]{1,0:T(8,128)(2,1)} custom-call(bf16[512,576]{1,0:T(8,128)(2,1)} %pad_maximum_fusion.2.r_0_, bf16[3,512,512]{2,1,0:T(8,128)(2,1)} %get-tuple-element.43.r_1_, bf16[512,192]{1,0:T(8,128)(2,1)} %copy.136.r_2_), custom_call_target="tpu_custom_call" | custom-call | tf_op jit(solution)/shard_map/cross_bwd/pallas_call | solution.py:439
  218.4 2.6 convolution_convert_fusion.4
  221.1 2.9 convolution_convert_fusion.3
  224.3 2.0 convolution_convert_fusion.2
  230.8 21.1 %exchange_4.1 = (bf16[512,768]{1,0:T(8,128)(2,1)}, f32[128,768]{1,0:T(8,128)}, f32[1,768]{1,0:T(1,128)}) custom-call(bf16[512,192]{1,0:T(8,128)(2,1)} %slice.232.refs_0_, bf16[768,192]{1,0:T(8,128)(2,1)} %get-tuple-element.122.refs_1_, f32[128,768]{1,0:T(8,128)} %get-tuple-element.39.stream_ref.refs_2_, f32[128,768]{1,0:T(8,128)} %get-tuple-element.45.refs_3_, ...), custom_call_target="tpu_custom_call" | custom-call | tf_op jit(solution)/shard_map/exchange_4/pallas_call | solution.py:282
  254.4 7.0 %self_bwd.1 = (bf16[512,576]{1,0:T(8,128)(2,1)}, f32[3,512]{1,0:T(4,128)}) custom-call(bf16[512,576]{1,0:T(8,128)(2,1)} %convolution_convert_fusion.5.r_0_, bf16[3,512,512]{2,1,0:T(8,128)(2,1)} %get-tuple-element.42.r_1_, bf16[512,192]{1,0:T(8,128)(2,1)} %copy.137.r_2_), custom_call_target="tpu_custom_call" | custom-call | tf_op jit(solution)/shard_map/self_bwd/pallas_call | solution.py:433
  262.5 15.7 %exchange_5.1 = (f32[128,768]{1,0:T(8,128)}, f32[1,768]{1,0:T(1,128)}) custom-call(bf16[512,576]{1,0:T(8,128)(2,1)} %get-tuple-element.47.refs_0_, bf16[768,576]{1,0:T(8,128)(2,1)} %slice.205.refs_1_, bf16[128,768]{1,0:T(8,128)(2,1)} %refs_2_.1, f32[128,768]{1,0:T(8,128)} %get-tuple-element.48.refs_3_, f32[1,768]{1,0:T(1,128)} %get-tuple-element.136.refs_4_), custom_call_target="tpu_custom_call" | custom-call | tf_op jit(solution)/shard_map/exchange_5/pallas_call | solution.py:282
  278.2 2.0 fusion.3
  282.8 2.5 copy.138
  286.4 76.5 %sum_over_dp.1 = (f32[96,1536]{1,0:T(8,128)}, f32[2,8,128]{2,1,0:T(8,128)}) custom-call(bf16[8,96,1536]{2,1,0:T(8,128)(2,1)} %bitcast.59, f32[8,8,128]{2,1,0:T(8,128)} %fusion.28.small_ref), custom_call_target="tpu_custom_call" | custom-call | tf_op jit(solution)/shard_map/sum_over_dp/pallas_call | solution.py:395
  362.9 2.2 slice_bitcast_fusion.1
  372.7 21.9 %reduce-scatter.8.cloned.1.call-done = bf16[96,1536]{1,0:T(8,128)(2,1)} async-done(((bf16[768,1536]{1,0:T(8,128)(2,1)}), bf16[96,1536]{1,0:T(8,128)(2,1)}) %reduce-scatter.8.cloned.1.call-update) | async-done | bytes 294928 | tf_op jit(solution)/shard_map/reduce_scatter | solution.py:449
  (144 shorter events, 45.3 us)
Async XLA Ops:
  7.2 7.4 %copy-start = (f32[32,3]{0,1:T(4,128)S(1)}, f32[32,3]{0,1:T(4,128)}, u32[]{:S(2)}) copy-start(f32[32,3]{0,1:T(4,128)} %param.35) | copy-start | bytes 1156
  7.2 7.4 %copy-start.17 = (f32[32,512]{1,0:T(8,128)S(1)}, f32[32,512]{1,0:T(8,128)}, u32[]{:S(2)}) copy-start(f32[32,512]{1,0:T(8,128)} %constant.32.clone) | copy-start | bytes 196612
  7.2 6.5 %copy-start.10 = (bf16[128,768]{1,0:T(8,128)(2,1)S(1)}, bf16[128,768]{1,0:T(8,128)(2,1)}, u32[]{:S(2)}) copy-start(bf16[128,768]{1,0:T(8,128)(2,1)} %refs_3_.1) | copy-start | bytes 589828
  7.2 6.5 %copy-start.19 = (bf16[128,768]{1,0:T(8,128)(2,1)S(1)}, bf16[128,768]{1,0:T(8,128)(2,1)}, u32[]{:S(2)}) copy-start(bf16[128,768]{1,0:T(8,128)(2,1)} %param.20) | copy-start | bytes 589828
  7.2 9.3 %copy-start.4 = (bf16[128,768]{1,0:T(8,128)(2,1)S(1)}, bf16[128,768]{1,0:T(8,128)(2,1)}, u32[]{:S(2)}) copy-start(bf16[128,768]{1,0:T(8,128)(2,1)} %refs_2_.1) | copy-start | bytes 589828
  7.2 53.9 %all-gather.8.cloned.1.call-start = ((), (), s32[]{:S(2)}) async-start(), calls=%async_computation.5 | async-start | bytes 2654208 | tf_op jit(solution)/shard_map/all_gather | solution.py:445
  9.2 107.0 %all-gather.4.cloned.1.call-start = ((), (), s32[]{:S(2)}) async-start(), calls=%async_computation.3 | async-start | bytes 2875392 | tf_op jit(solution)/shard_map/all_gather | solution.py:445
  13.7 138.4 %all-gather.6.cloned.1.call-start = ((), (), s32[]{:S(2)}) async-start(), calls=%async_computation.4 | async-start | bytes 1966080 | tf_op jit(solution)/shard_map/all_gather | solution.py:61
  14.5 354.8 %reduce-scatter.6.cloned.1.call-start = ((), (), s32[]{:S(2)}) async-start(), calls=%async_computation.7 | async-start | bytes 983040 | tf_op jit(solution)/shard_map/reduce_scatter | solution.py:65
  117.9 9.9 %copy-start.1 = (bf16[768,1539]{1,0:T(8,128)(2,1)S(1)}, bf16[768,1539]{1,0:T(8,128)(2,1)}, u32[]{:S(2)}) copy-start(bf16[768,1539]{1,0:T(8,128)(2,1)} %all-gather.4.cloned.1.call-done) | copy-start | bytes 7091716
  180.9 2.8 copy-start.24
  221.1 149.9 %reduce-scatter.4.cloned.1.call-start = ((), (), s32[]{:S(2)}) async-start(), calls=%async_computation.6 | async-start | bytes 983040 | tf_op jit(solution)/shard_map/reduce_scatter | solution.py:65
  224.0 170.5 %reduce-scatter.8.cloned.1.call-start = ((), (), s32[]{:S(2)}) async-start(), calls=%async_computation.8 | async-start | bytes 2654208 | tf_op jit(solution)/shard_map/reduce_scatter | solution.py:449
  224.3 2.0 copy-start.13
  224.3 2.0 copy-start.15
  278.2 2.4 copy-start.6
  278.2 2.4 copy-start.11
  282.7 2.5 copy-start.21
  282.7 2.5 copy-start.22
  282.8 2.5 copy-start.23
  282.8 2.6 copy-start.18
  282.8 2.6 copy-start.20
  286.4 84.6 %copy-start.5 = (f32[128,768]{1,0:T(8,128)S(1)}, f32[128,768]{1,0:T(8,128)}, u32[]{:S(2)}) copy-start(f32[128,768]{1,0:T(8,128)} %get-tuple-element.40.refs_2_) | copy-start | bytes 1179652
  365.0 32.3 %copy-start.16 = (f32[128,768]{1,0:T(8,128)S(1)}, f32[128,768]{1,0:T(8,128)}, u32[]{:S(2)}) copy-start(f32[128,768]{1,0:T(8,128)} %get-tuple-element.158) | copy-start | bytes 1179652
  (9 other events, 15.6 us)
Sparse Core Ops, SparseCore 0:
  10.2 50.8 all-gather.7
  63.9 52.1 all-gather.3
  118.3 21.6 all-gather.5
  221.2 24.8 reduce-scatter.5
  248.5 29.9 reduce-scatter.3
  281.8 112.6 reduce-scatter.7

commit v3 on v2

--- a/solution.py
+++ b/solution.py
@@ -482,22 +482,27 @@
         wq_self, wk_self, wv_self, wo_self.T, wq_cross, wk_cross, wv_cross, wo_cross.T, norm_scales.T
     )
     stream_all = spread(layer_in)
-    others = spread(jnp.concatenate([encoder_states, grad_out], axis=1))
-    second = gather_weights(w_gate, w_up, w_down.T)
+    first, stream_all, others = lax.optimization_barrier(
+        (first, stream_all, jnp.concatenate([encoder_states, grad_out], axis=1))
+    )
+    others = spread(others)
     self_qkv_w = first[:, :3 * W]
     self_out_t = first[:, 3 * W:4 * W]
     cross_q_w = first[:, 4 * W:5 * W]
     cross_kv_w = first[:, 5 * W:7 * W]
     cross_out_t = first[:, 7 * W:8 * W]
     gains = first[:, 8 * W:].T.astype(F32)
+    rows_one = to_half(unit_norm(stream_all.astype(F32))[0] * gains[0:1])
+    self_qkv = to_half(matmul(rows_one, self_qkv_w))
+    mixed_self, probs_self = attend(self_qkv, base, keep[0])
+    mixed_self, others, feed_parts = lax.optimization_barrier(
+        (mixed_self, others, jnp.concatenate([w_gate, w_up, w_down.T], axis=1))
+    )
+    second = gather_weights(feed_parts)
     gate_up_w = second[:, :2 * FFL]
     down_t = second[:, 2 * FFL:]
     source_rows = others[:, :D]
     grad_rows = others[:, D:]
-
-    rows_one = to_half(unit_norm(stream_all.astype(F32))[0] * gains[0:1])
-    self_qkv = to_half(matmul(rows_one, self_qkv_w))
-    mixed_self, probs_self = attend(self_qkv, base, keep[0])
     rows_two, stream_one = forward_exchange(1, mixed_self, self_out_t, layer_in, gains[1:2])
     cross_qkv = jnp.concatenate(
         [to_half(matmul(rows_two, cross_q_w)), to_half(matmul(source_rows, cross_kv_w))], axis=1
@@ -518,7 +523,6 @@
     grad_third = scatter_grads(
         left_contract(rows_three, grad_gate_up), left_contract(grad_rows, hidden)
     )
-    layer_out = to_half(stream_two + collect(right_contract(hidden, down_t)))
     grad_mixed_cross = to_half(matmul(grad_two_rows, cross_out_t))
     grad_cross = attend_back(cross_qkv, probs_cross, grad_mixed_cross, False)
     grad_q_cross = grad_cross[:, :W]
@@ -526,9 +530,18 @@
     grad_one_rows, grad_stream_one, gain_two = backward_exchange(
         4, True, grad_q_cross, cross_q_w, stream_one, grad_stream_two, gains[1:2]
     )
-    grad_encoder = collect(right_contract(grad_kv_cross, cross_kv_w))
     grad_mixed_self = to_half(matmul(grad_one_rows, self_out_t))
     grad_self, diagonal = attend_back(self_qkv, probs_self, grad_mixed_self, True)
+    hidden_late, grad_kv_late, grad_third, _ = lax.optimization_barrier(
+        (hidden, grad_kv_cross, grad_third, grad_self)
+    )
+    late_rows = collect(
+        jnp.concatenate(
+            [right_contract(hidden_late, down_t), right_contract(grad_kv_late, cross_kv_w)], axis=1
+        )
+    )
+    layer_out = to_half(stream_two + late_rows[:, :D])
+    grad_encoder = late_rows[:, D:]
     grad_in, gain_one = backward_exchange(
         5, False, grad_self, self_qkv_w, layer_in, grad_stream_one, gains[0:1]
     )

time: 410 us -> 323 us (0.79); the launches traced: 405 us -> 322 us
  waiting for transfers between devices: 109 us -> 47.9 us
  Pallas kernels: 201 us -> 178 us
  local copies, waits for them, and re-layouts: 29 us -> 35.8 us
  matrix products: 28.4 us -> 23 us
    all_gather x2, waiting for transfers between devices: 87.5 us -> 42.5 us  [gather_weights(): lax.all_gather(jnp.concatenate(parts, axis=1), 'dp', axis=0, tiled=True)]
    reduce_scatter x1, waiting for transfers between devices: 21.9 us -> 0.08 us  [scatter_grads(): lax.psum_scatter(to_half(jnp.concatenate(parts, axis=1)), 'dp', scatter_d...]
    pallas_call x1, Pallas kernels: 76.5 us -> 58.1 us  [sum_over_dp(): pl.pallas_call(sum_kernel, out_shape=(whole((rows, width), F32), whole((2...]
    all_gather x1, waiting for transfers between devices: 0.01 us -> 5.19 us  [spread(): return lax.all_gather(rows_local, 'tensor', axis=0, tiled=True)]
    pallas_call x5, Pallas kernels: 96.2 us -> 91.5 us  [exchange(): pl.pallas_call(kernel, out_shape=outs, scratch_shapes=scratch, name=f'exc...]
    optimization_barrier x0 -> x1, local copies, waits for them, and re-layouts: none -> 4.64 us  [per_device(): lax.optimization_barrier((first, stream_all, jnp.concatenate([encoder_sta...]
  transfers between devices with their start and end apart: 6 -> 5, of which waited for: 3 -> 4; matrix products, arithmetic and copies ran while one was open for 12% -> 15% of each run, Pallas kernels for 36% -> 55%
where the time goes in v3:
time: 323 us; the launch traced here: 322 us
  Pallas kernels  178 us (55%)
  waiting for transfers between devices  47.9 us (15%)
  local copies, waits for them, and re-layouts  35.8 us (11%)
  matrix products  23 us (7%)
  between operations  14.4 us (4%)
  other arithmetic  13.6 us (4%)
  blocking collectives  9.1 us (3%)
    pallas_call x5, Pallas kernels, exchange(): pl.pallas_call(kernel, out_shape=outs, scratch_shapes=scratch, name=f'exc...  91.5 us
    pallas_call x1, Pallas kernels, sum_over_dp(): pl.pallas_call(sum_kernel, out_shape=(whole((rows, width), F32), whole((2...  58.1 us
    all_gather x2, waiting for transfers between devices, gather_weights(): lax.all_gather(jnp.concatenate(parts, axis=1), 'dp', axis=0, tiled=True)  42.5 us
    dot_general x7, matrix products, matmul(): return jnp.dot(left_side, right_side, preferred_element_type=F32)  13.6 us
    all_gather x1, blocking collectives, spread(): return lax.all_gather(rows_local, 'tensor', axis=0, tiled=True)  9.1 us
    pallas_call x1, Pallas kernels, attend_back(): call(lambda *r: attend_back_kernel(False, *r), grads, scratch, name='cros...  7.47 us
    unnamed x71, local copies, waits for them, and re-layouts  7.39 us
    pallas_call x1, Pallas kernels, attend_back(): call(lambda *r: attend_back_kernel(True, *r), (grads, whole((width // DH,...  7.06 us
  transfers between devices with their start and end apart: 5, of which 4 were waited for; matrix products, arithmetic and copies ran while one was open for 15% of the time, Pallas kernels for 55%

profile of v3, /device:TPU:13, one launch (start us, length us, event | category | flops | bytes accessed | tf_op | source)
XLA Modules:
  0.0 322.1 jit_solution(11996900214501276227)
XLA Ops:
  13.7 9.1 %all_gather.13 = bf16[512,768]{1,0:T(8,128)(2,1)S(1)} all-gather(bf16[128,768]{1,0:T(8,128)(2,1)S(1)} %copy-done.6), channel_id=1, replica_groups=mesh['dp'=8,'tensor'=4] {'tensor'}, dimensions={0}, use_global_device_ids=true | all-gather | bytes 983040 | tf_op jit(solution)/shard_map/all_gather | solution.py:61
  22.8 42.0 %all-gather.4.cloned.1.call-done = bf16[768,1539]{1,0:T(8,128)(2,1)} async-done(((bf16[96,1539]{1,0:T(8,128)(2,1)}), bf16[768,1539]{1,0:T(8,128)(2,1)}) %all-gather.4.cloned.1.call-update) | async-done | bytes 2363920 | tf_op jit(solution)/shard_map/all_gather | solution.py:445
  67.5 4.6 %copy.123 = bf16[768,1539]{0,1:T(8,128)(2,1)} copy(bf16[768,1539]{1,0:T(8,128)(2,1)} %all-gather.4.cloned.1.call-done) | data formatting | bytes 4727808 | tf_op jit(solution)/shard_map/optimization_barrier | solution.py:485
  75.4 6.9 %self_fwd.1 = (bf16[512,192]{1,0:T(8,128)(2,1)}, bf16[3,512,512]{2,1,0:T(8,128)(2,1)}) custom-call(bf16[512,576]{1,0:T(8,128)(2,1)} %convolution_convert_fusion.5.r_0_, f32[3,8,512]{2,1,0:T(8,128)} %stack.35.r_1_, s32[512,512]{1,0:T(8,128)} %bitcast.62), custom_call_target="tpu_custom_call" | custom-call | tf_op jit(solution)/shard_map/self_fwd/pallas_call | solution.py:425
  82.4 5.2 %all-gather.6.cloned.1.call-done = bf16[512,1536]{1,0:T(8,128)(2,1)} async-done(((bf16[128,1536]{1,0:T(8,128)(2,1)}), bf16[512,1536]{1,0:T(8,128)(2,1)}) %all-gather.6.cloned.1.call-update) | async-done | bytes 1572880 | tf_op jit(solution)/shard_map/all_gather | solution.py:61
  89.1 18.2 %exchange_1.1 = (bf16[512,768]{1,0:T(8,128)(2,1)}, f32[128,768]{1,0:T(8,128)}) custom-call(bf16[512,192]{1,0:T(8,128)(2,1)} %get-tuple-element.49.lhs_ref, bf16[768,192]{1,0:T(8,128)(2,1)} %get-tuple-element.142.w_ref, bf16[128,768]{1,0:T(8,128)(2,1)} %refs_2_.1, f32[1,768]{1,0:T(1,128)} %get-tuple-element.158.gain_ref.refs_4_), custom_call_target="tpu_custom_call" | custom-call | tf_op jit(solution)/shard_map/exchange_1/pallas_call | solution.py:282
  109.7 1.8 convolution_convert_fusion.7
  112.7 6.8 %cross_fwd.1 = (bf16[512,192]{1,0:T(8,128)(2,1)}, bf16[3,512,512]{2,1,0:T(8,128)(2,1)}) custom-call(bf16[512,576]{1,0:T(8,128)(2,1)} %pad_maximum_fusion.3.r_0_), custom_call_target="tpu_custom_call" | custom-call | tf_op jit(solution)/shard_map/cross_fwd/pallas_call | solution.py:424
  119.5 19.1 %exchange_2.1 = (bf16[512,768]{1,0:T(8,128)(2,1)}, f32[128,768]{1,0:T(8,128)}) custom-call(bf16[512,192]{1,0:T(8,128)(2,1)} %get-tuple-element.52.lhs_ref, bf16[768,192]{1,0:T(8,128)(2,1)} %get-tuple-element.141.w_ref, f32[128,768]{1,0:T(8,128)} %get-tuple-element.53.stream_ref.refs_2_, f32[1,768]{1,0:T(1,128)} %get-tuple-element.157.gain_ref.refs_4_), custom_call_target="tpu_custom_call" | custom-call | tf_op jit(solution)/shard_map/exchange_2/pallas_call | solution.py:282
  139.2 2.7 fusion.34
  141.9 2.3 fusion.14
  148.9 2.8 slice.229.refs_1_
  152.8 22.3 %exchange_3.1 = (bf16[512,768]{1,0:T(8,128)(2,1)}, f32[128,768]{1,0:T(8,128)}, f32[1,768]{1,0:T(1,128)}) custom-call(bf16[512,1024]{1,0:T(8,128)(2,1)} %pad_maximum_fusion.2.refs_0_, bf16[768,1024]{1,0:T(8,128)(2,1)} %slice.229.refs_1_, f32[128,768]{1,0:T(8,128)} %get-tuple-element.54.refs_2_, bf16[128,768]{1,0:T(8,128)(2,1)} %refs_3_.1, ...), custom_call_target="tpu_custom_call" | custom-call | tf_op jit(solution)/shard_map/exchange_3/pallas_call | solution.py:282
  177.7 7.5 %cross_bwd.1 = bf16[512,576]{1,0:T(8,128)(2,1)} custom-call(bf16[512,576]{1,0:T(8,128)(2,1)} %pad_maximum_fusion.3.r_0_, bf16[3,512,512]{2,1,0:T(8,128)(2,1)} %get-tuple-element.57.r_1_, bf16[512,192]{1,0:T(8,128)(2,1)} %copy.136.r_2_), custom_call_target="tpu_custom_call" | custom-call | tf_op jit(solution)/shard_map/cross_bwd/pallas_call | solution.py:439
  185.2 2.0 slice.233
  188.8 18.3 %exchange_4.1 = (bf16[512,768]{1,0:T(8,128)(2,1)}, f32[128,768]{1,0:T(8,128)}, f32[1,768]{1,0:T(1,128)}) custom-call(bf16[512,192]{1,0:T(8,128)(2,1)} %slice.234.refs_0_, bf16[768,192]{1,0:T(8,128)(2,1)} %get-tuple-element.140.refs_1_, f32[128,768]{1,0:T(8,128)} %get-tuple-element.53.stream_ref.refs_2_, f32[128,768]{1,0:T(8,128)} %get-tuple-element.60.refs_3_, ...), custom_call_target="tpu_custom_call" | custom-call | tf_op jit(solution)/shard_map/exchange_4/pallas_call | solution.py:282
  209.7 7.1 %self_bwd.1 = (bf16[512,576]{1,0:T(8,128)(2,1)}, f32[3,512]{1,0:T(4,128)}) custom-call(bf16[512,576]{1,0:T(8,128)(2,1)} %convolution_convert_fusion.5.r_0_, bf16[3,512,512]{2,1,0:T(8,128)(2,1)} %get-tuple-element.59.r_1_, bf16[512,192]{1,0:T(8,128)(2,1)} %copy.138.r_2_), custom_call_target="tpu_custom_call" | custom-call | tf_op jit(solution)/shard_map/self_bwd/pallas_call | solution.py:433
  216.8 1.9 convert_element_type.70
  218.7 1.9 convolution_convert_fusion.4
  224.9 13.5 %exchange_5.1 = (f32[128,768]{1,0:T(8,128)}, f32[1,768]{1,0:T(1,128)}) custom-call(bf16[512,576]{1,0:T(8,128)(2,1)} %get-tuple-element.62.refs_0_, bf16[768,576]{1,0:T(8,128)(2,1)} %slice.167.refs_1_, bf16[128,768]{1,0:T(8,128)(2,1)} %refs_2_.1, f32[128,768]{1,0:T(8,128)} %get-tuple-element.65.refs_3_, f32[1,768]{1,0:T(1,128)} %get-tuple-element.155.refs_4_), custom_call_target="tpu_custom_call" | custom-call | tf_op jit(solution)/shard_map/exchange_5/pallas_call | solution.py:282
  238.4 2.0 fusion.3
  243.0 2.5 copy.139
  246.7 58.1 %sum_over_dp.1 = (f32[96,1536]{1,0:T(8,128)}, f32[2,8,128]{2,1,0:T(8,128)}) custom-call(bf16[8,96,1536]{2,1,0:T(8,128)(2,1)} %bitcast.61, f32[8,8,128]{2,1,0:T(8,128)} %fusion.27.small_ref), custom_call_target="tpu_custom_call" | custom-call | tf_op jit(solution)/shard_map/sum_over_dp/pallas_call | solution.py:395
  304.8 2.2 slice_bitcast_fusion.1
  (154 shorter events, 46.9 us)
Async XLA Ops:
  7.2 57.6 %copy-start = (f32[32,3]{0,1:T(4,128)S(1)}, f32[32,3]{0,1:T(4,128)}, u32[]{:S(2)}) copy-start(f32[32,3]{0,1:T(4,128)} %param.35) | copy-start | bytes 1156
  7.2 57.6 %copy-start.18 = (f32[32,512]{1,0:T(8,128)S(1)}, f32[32,512]{1,0:T(8,128)}, u32[]{:S(2)}) copy-start(f32[32,512]{1,0:T(8,128)} %constant.32.clone) | copy-start | bytes 196612
  7.2 6.5 %copy-start.6 = (bf16[128,768]{1,0:T(8,128)(2,1)S(1)}, bf16[128,768]{1,0:T(8,128)(2,1)}, u32[]{:S(2)}) copy-start(bf16[128,768]{1,0:T(8,128)(2,1)} %refs_2_.1) | copy-start | bytes 589828
  7.2 59.6 %copy-start.20 = (bf16[512,96]{0,1:T(8,128)(2,1)S(1)}, bf16[512,96]{0,1:T(8,128)(2,1)}, u32[]{:S(2)}) copy-start(bf16[512,96]{0,1:T(8,128)(2,1)} %param.33) | copy-start | bytes 294916
  7.2 59.6 %copy-start.21 = (bf16[96,512]{1,0:T(8,128)(2,1)S(1)}, bf16[96,512]{1,0:T(8,128)(2,1)}, u32[]{:S(2)}) copy-start(bf16[96,512]{1,0:T(8,128)(2,1)} %param.32) | copy-start | bytes 294916
  7.2 59.6 %copy-start.22 = (bf16[96,512]{1,0:T(8,128)(2,1)S(1)}, bf16[96,512]{1,0:T(8,128)(2,1)}, u32[]{:S(2)}) copy-start(bf16[96,512]{1,0:T(8,128)(2,1)} %param.31) | copy-start | bytes 294916
  7.3 57.5 %all-gather.4.cloned.1.call-start = ((), (), s32[]{:S(2)}) async-start(), calls=%async_computation.2 | async-start | bytes 2875392 | tf_op jit(solution)/shard_map/all_gather | solution.py:445
  11.8 75.7 %all-gather.6.cloned.1.call-start = ((), (), s32[]{:S(2)}) async-start(), calls=%async_computation.3 | async-start | bytes 1966080 | tf_op jit(solution)/shard_map/all_gather | solution.py:61
  64.7 74.4 %all-gather.8.cloned.1.call-start = ((), (), s32[]{:S(2)}) async-start(), calls=%async_computation.4 | async-start | bytes 2654208 | tf_op jit(solution)/shard_map/all_gather | solution.py:445
  67.5 6.2 %copy-start.1 = (bf16[768,1539]{1,0:T(8,128)(2,1)S(1)}, bf16[768,1539]{1,0:T(8,128)(2,1)}, u32[]{:S(2)}) copy-start(bf16[768,1539]{1,0:T(8,128)(2,1)} %all-gather.4.cloned.1.call-done) | copy-start | bytes 7091716
  87.6 129.3 %reduce-scatter.3.cloned.1.call-start = ((), (), s32[]{:S(2)}) async-start(), calls=%async_computation.5 | async-start | bytes 2654208 | tf_op jit(solution)/shard_map/reduce_scatter | solution.py:449
  139.2 2.8 copy-start.27
  148.6 163.5 %reduce-scatter.5.cloned.1.call-start = ((), (), s32[]{:S(2)}) async-start(), calls=%async_computation.6 | async-start | bytes 1966080 | tf_op jit(solution)/shard_map/reduce_scatter | solution.py:65
  148.9 2.8 copy-start.14
  148.9 2.8 copy-start.16
  216.8 3.8 %copy-start.31 = (bf16[512,512]{1,0:T(8,128)(2,1)S(1)}, bf16[512,512]{1,0:T(8,128)(2,1)}, u32[]{:S(2)}) copy-start(bf16[512,512]{1,0:T(8,128)(2,1)} %copy-done.30) | copy-start | bytes 1572868
  243.0 2.5 copy-start.24
  243.0 2.5 copy-start.25
  243.0 2.5 copy-start.26
  243.0 2.6 copy-start.19
  243.0 2.6 copy-start.23
  246.6 64.7 %copy-start.5 = (f32[96,1536]{1,0:T(8,128)S(1)}, f32[96,1536]{1,0:T(8,128)}, u32[]{:S(2)}) copy-start(f32[96,1536]{1,0:T(8,128)} %convert_element_type.70) | copy-start | bytes 1769476
  304.8 8.5 %copy-start.7 = (f32[128,768]{1,0:T(8,128)S(1)}, f32[128,768]{1,0:T(8,128)}, u32[]{:S(2)}) copy-start(f32[128,768]{1,0:T(8,128)} %get-tuple-element.54.refs_2_) | copy-start | bytes 1179652
  308.5 6.3 %copy-start.17 = (f32[128,768]{1,0:T(8,128)S(1)}, f32[128,768]{1,0:T(8,128)}, u32[]{:S(2)}) copy-start(f32[128,768]{1,0:T(8,128)} %get-tuple-element.176) | copy-start | bytes 1179652
  (13 other events, 22.1 us)
Sparse Core Ops, SparseCore 0:
  11.9 52.7 all-gather.3
  66.9 20.6 all-gather.5
  89.7 49.3 all-gather.7
  148.7 68.0 reduce-scatter.2
  223.8 29.1 reduce-scatter.4
